TPU v7x, 1024 devices: a whole 8x8x8 slice. The times are simulated.
1024 devices in a mesh: mom: 16 (over x, y_lo), en: 64 (over z, y_hi, core).
Axes of the slice: x: 8, y: 8 (y_hi: 4, y_lo: 2; y = y_hi * 2 + y_lo), z: 8, core: 2. Of those that a mesh axis runs over, the one named last changes fastest.
Arguments:
- retarded: bfloat16 [16, 64, 2, 768, 768], P('mom', 'en'), may hold values from -0.21875 to 0.21875
- injection: bfloat16 [16, 64, 2, 12, 768], P('mom', 'en'), may hold values from -6 to 6
- neighbours: int32 [64, 4], replicated, may hold values from 0 to 63, as said below
- bond_count: int32 [64], P('en'), may hold values from 1 to 4, as said below
- bond_mode: int32 [64, 4], P('en'), may hold values from 0 to 5
- mode_shift: int32 [6], replicated, may hold values from 1 to 8
- occupation: float32 [16, 6], replicated, may hold values from 0.1 to 4
- coupling: float32 [64, 4, 12, 12], P('en'), may hold values from -1.2 to 1.2
Outputs:
- scattering: float32 [16, 64, 64, 4, 144], P('mom', 'en')
Inputs may be any that keep to these rules, and one draw needn't show every extreme that they name: `neighbours`: each row lists 4 different atoms, none equal to the row's own atom; only the first bond_count entries of a row are bonds. `bond_count`: some atom has 4 bonds.
All inputs are finite; a program needn't handle non-finite values.
Results may differ from a plain program's by a relative error of at most 0.0049.
Values may be sent and summed in bfloat16 or wider, within the bound.
No kernel may reach another device: no remote copies, remote signals or barrier semaphores. Data moves between devices by JAX's collectives and lax.ppermute only.
A program may use at most 32 MiB of HBM per device.

v0:
```python
import jax
import jax.numpy as jnp
from jax import lax
from jax.sharding import Mesh
from jax.sharding import PartitionSpec as P

EN = ("en_0", "en_1", "en_2")


def split_up(x, dim, peers):
    dims = x.shape
    blocks = x.reshape(*dims[:dim], peers, dims[dim] // peers, *dims[dim + 1 :])
    return jnp.moveaxis(blocks, dim, 0)


def joined_along(blocks, dim):
    dims = list(blocks.shape[1:])
    dims[dim] *= blocks.shape[0]
    return jnp.moveaxis(blocks, 0, dim).reshape(dims)


def turned_blocks(blocks, axes, turns):
    dims = [lax.axis_size(a) for a in axes]
    blocks = blocks.reshape(*dims, *blocks.shape[1:])
    for k in turns:
        blocks = lax.all_to_all(blocks, axes[k], split_axis=k, concat_axis=k, tiled=True)
    return blocks.reshape(-1, *blocks.shape[len(axes) :])


def exchange_by_chip(x, groups, turns, split_dim, concat_dim):
    peers = lax.axis_size(groups[0]) * lax.axis_size(groups[1])
    blocks = split_up(x, split_dim, peers)
    return joined_along(turned_blocks(blocks, groups, turns), concat_dim)


def from_behind(block, axis, distance):
    devices = range(lax.axis_size(axis))
    route = [((i - distance) % len(devices), i) for i in devices]
    return lax.ppermute(block, axis, route)


def dense_product(former, latter):
    return jnp.einsum("erq,eqk->erk", former, latter, preferred_element_type=jnp.float32)


def row_product(former, latter):
    return jnp.einsum("ebic,ebkc->ebik", former, latter, preferred_element_type=jnp.float32)


def diagonal_pick(rows, selector):
    return jnp.einsum("ebic,bkc->ebik", rows, selector, preferred_element_type=jnp.float32)


def complex_blocks(retarded, injection):
    energy_dev = retarded.shape[1]
    order = retarded.shape[3]
    orbital = injection.shape[3]
    atom_count = order // orbital
    real_part = retarded[0, :, 0]
    imag_part = retarded[0, :, 1]
    row_atom = jnp.arange(order, dtype=jnp.int32) // orbital
    same_atom = row_atom[:, None] == row_atom[None, :]
    zero_block = jnp.zeros((), jnp.bfloat16)
    s_real = jnp.where(
        same_atom[None], jnp.tile(injection[0, :, 0], (1, atom_count, 1)), zero_block
    )
    s_imag = jnp.where(
        same_atom[None], jnp.tile(injection[0, :, 1], (1, atom_count, 1)), zero_block
    )
    left_real = (dense_product(real_part, s_real) - dense_product(imag_part, s_imag)).astype(
        jnp.bfloat16
    )
    left_imag = (dense_product(real_part, s_imag) + dense_product(imag_part, s_real)).astype(
        jnp.bfloat16
    )
    left_real = left_real.reshape(energy_dev, atom_count, orbital, order)
    left_imag = left_imag.reshape(energy_dev, atom_count, orbital, order)
    real_rows = real_part.reshape(energy_dev, atom_count, orbital, order)
    imag_rows = imag_part.reshape(energy_dev, atom_count, orbital, order)
    lesser_real = row_product(left_real, real_rows) + row_product(left_imag, imag_rows)
    lesser_imag = row_product(left_imag, real_rows) - row_product(left_real, imag_rows)
    column_index = jnp.arange(order, dtype=jnp.int32)
    wanted = (
        jnp.arange(atom_count, dtype=jnp.int32)[:, None] * orbital
        + jnp.arange(orbital, dtype=jnp.int32)[None, :]
    )
    selector = (column_index[None, None, :] == wanted[:, :, None]).astype(jnp.bfloat16)
    diag_real = diagonal_pick(real_rows, selector)
    diag_imag = diagonal_pick(imag_rows, selector)
    greater_real = lesser_real + diag_real - jnp.swapaxes(diag_real, 2, 3)
    greater_imag = lesser_imag + diag_imag + jnp.swapaxes(diag_imag, 2, 3)
    stacked = jnp.stack([lesser_real, lesser_imag, greater_real, greater_imag], axis=2)
    return stacked.reshape(energy_dev, atom_count, 4 * orbital * orbital).astype(jnp.bfloat16)


def per_device(
    retarded, injection, neighbours, bond_count, bond_mode, mode_shift, occupation, coupling
):
    blocks = complex_blocks(retarded, injection)
    atom_count = neighbours.shape[0]
    select = (
        neighbours[:, :, None] == jnp.arange(atom_count, dtype=jnp.int32)[None, None, :]
    ).astype(jnp.bfloat16)
    outgoing = jnp.einsum(
        "amb,ebx->aemx", select, blocks, preferred_element_type=jnp.float32
    ).astype(jnp.bfloat16)
    received = exchange_by_chip(outgoing, (("en_0", "en_1"), "en_2"), (1, 0), 0, 1)
    atom_dev, energies, bond_slots = (received.shape[0], received.shape[1], received.shape[2])
    orbital = coupling.shape[2]
    entries = orbital * orbital
    n_modes = mode_shift.shape[0]
    kron_pair = (
        (coupling[:, :, :, None, :, None] * coupling[:, :, None, :, None, :])
        .reshape(atom_dev, bond_slots, entries, entries)
        .astype(jnp.bfloat16)
    )
    mode_pick = bond_mode[:, :, None] == jnp.arange(n_modes, dtype=jnp.int32)[None, None, :]
    shift_bond = jnp.sum(jnp.where(mode_pick, mode_shift[None, None, :], 0), axis=-1)
    energy_index = jnp.arange(energies, dtype=jnp.int32)
    target_e = energy_index[None, None, :, None]
    source_e = energy_index[None, None, None, :]
    lower_map = (source_e == target_e - shift_bond[:, :, None, None]).astype(jnp.float32)
    upper_map = (source_e == target_e + shift_bond[:, :, None, None]).astype(jnp.float32)
    bond_live = (jnp.arange(bond_slots, dtype=jnp.int32)[None, :] < bond_count[:, None]).astype(
        jnp.float32
    )
    greater = jnp.array([0.0, 0.0, 1.0, 1.0], dtype=jnp.float32)
    momenta = lax.axis_size("mom")

    def weighted(imaged, transfer):
        occupied_row = lax.dynamic_index_in_dim(occupation, transfer, 0, keepdims=False)
        occupied = jnp.sum(jnp.where(mode_pick, occupied_row[None, None, :], 0.0), axis=-1)
        weight_low = bond_live[:, :, None] * (occupied[:, :, None] + greater[None, None, :])
        weight_high = bond_live[:, :, None] * (occupied[:, :, None] + 1.0 - greater[None, None, :])
        mixing = (
            weight_low[:, :, :, None, None] * lower_map[:, :, None]
            + weight_high[:, :, :, None, None] * upper_map[:, :, None]
        )
        return jnp.einsum(
            "amcef,amfcx->aecx",
            mixing,
            imaged,
            precision=lax.Precision.HIGHEST,
            preferred_element_type=jnp.float32,
        )

    empty_sum = jnp.zeros((atom_dev, energies, 4, entries), jnp.float32)
    pieces = received.reshape(atom_dev, energies, bond_slots, 4, entries)
    imaged = jnp.einsum("amij,aemcj->ameci", kron_pair, pieces, preferred_element_type=jnp.float32)

    def advance(turn_index, running):
        running = running + weighted(imaged, momenta - 1 - turn_index)
        return from_behind(running, "mom", 1)

    running = lax.fori_loop(0, momenta - 1, advance, empty_sum)
    running = running + weighted(imaged, 0)
    return (running / momenta)[None]


def solution(mesh):
    split = Mesh(mesh.devices.reshape(mesh.shape["mom"], 8, 4, 2), ("mom", "en_0", "en_1", "en_2"))
    in_specs = (
        P("mom", EN, None, None, None),
        P("mom", EN, None, None, None),
        P(),
        P(EN),
        P(EN, None),
        P(),
        P(),
        P(EN, None, None, None),
    )
    out_specs = P("mom", EN, None, None, None)
    return jax.shard_map(
        per_device, mesh=split, in_specs=in_specs, out_specs=out_specs, check_vma=False
    )
```

profile of v0, /device:TPU:8, one launch (start us, length us, event | category | flops | bytes accessed | tf_op | source)
XLA Modules:
  0.0 282.3 jit_solution(8824297026365215904)
XLA Ops:
  2.7 3.4 %fusion.62 = (bf16[1,1,1,768,768]{4,3,2,1,0:T(8,128)(2,1)}, bf16[1,1,1,768,768]{4,3,2,1,0:T(8,128)(2,1)}) fusion(bf16[1,1,2,768,768]{4,3,2,1,0:T(8,128)(2,1)} %param.11), kind=kLoop, calls=%fused_computation.110 | loop fusion | bytes 4718592 | tf_op jit(solution)/shard_map/slice | solution.py:59
  8.9 3.9 %fusion.29 = f32[768,768]{0,1:T(8,128)} fusion(bf16[768,768]{1,0:T(8,128)(2,1)S(1)} %select_n.125, bf16[1,1,2,768,768]{4,3,2,1,0:T(8,128)(2,1)} %param.11), kind=kOutput, calls=%fused_computation.46 | convolution fusion | flops 905969664 | bytes 4718592 | tf_op jit(solution)/shard_map/erq,eqk->erk/dot_general | solution.py:43
  19.4 4.5 %fusion.23 = bf16[768,768]{1,0:T(8,128)(2,1)} fusion(f32[768,768]{0,1:T(8,128)} %fusion.29, bf16[768,768]{1,0:T(8,128)(2,1)} %select_n.123, bf16[1,1,2,768,768]{4,3,2,1,0:T(8,128)(2,1)} %param.11), kind=kOutput, calls=%fused_computation.37 | convolution fusion | flops 907149312 | bytes 5898240 | tf_op jit(solution)/shard_map/erq,eqk->erk/dot_general | solution.py:43
  23.9 3.1 %reshape.1008 = bf16[64,12,768]{2,1,0:T(8,128)(2,1)} reshape(bf16[768,768]{1,0:T(8,128)(2,1)} %fusion.23) | data formatting | bytes 2359296 | tf_op jit(solution)/shard_map/reshape.33
  27.0 3.1 %reshape.1009 = bf16[64,12,768]{2,1,0:T(8,128)(2,1)} reshape(bf16[1,1,1,768,768]{4,3,2,1,0:T(8,128)(2,1)} %get-tuple-element.331) | data formatting | bytes 2359296 | tf_op jit(solution)/shard_map/reshape.34
  43.1 4.0 %all_to_all.10 = bf16[32,2,1,1,4,576]{5,4,0,3,2,1:T(4,128)(2,1)S(1)} all-to-all(bf16[32,2,1,1,4,576]{5,4,0,3,2,1:T(4,128)(2,1)S(1)} %copy.56), channel_id=1, replica_groups=mesh['mom'=16,'en_0'=8,'en_1'=4,'en_2'=2] {'en_2'}, dimensions={1} | all-to-all | bytes 589824 | tf_op jit(solution)/shard_map/all_to_all | solution.py:26
  47.9 23.1 %all-to-all-start.1 = ((bf16[32,2,1,1,4,576]{5,4,1,3,2,0:T(4,128)(2,1)}), bf16[32,2,1,1,4,576]{5,4,1,3,2,0:T(4,128)(2,1)S(1)}, u32[]{:S(2)}, u32[]{:S(2)}) async-start(bf16[32,2,1,1,4,576]{5,4,1,3,2,0:T(4,128)(2,1)} %copy.57), calls=%async_computation.1 | async-start | bytes 655360 | tf_op jit(solution)/shard_map/all_to_all | solution.py:26
  75.0 11.5 %all-to-all-done.1 = bf16[32,2,1,1,4,576]{5,4,1,3,2,0:T(4,128)(2,1)S(1)} async-done(((bf16[32,2,1,1,4,576]{5,4,1,3,2,0:T(4,128)(2,1)}), bf16[32,2,1,1,4,576]{5,4,1,3,2,0:T(4,128)(2,1)S(1)}, u32[]{:S(2)}, u32[]{:S(2)}) %all-to-all-start.1) | async-done | bytes 294944 | tf_op jit(solution)/shard_map/all_to_all | solution.py:26
  87.4 193.2 %while.17 = (s32[]{:T(128)}, f32[1,64,4,144]{3,1,2,0:T(8,128)S(1)}, f32[16,6]{1,0:T(8,128)S(1)}, f32[1,4,64,4,144]{4,2,1,3,0:T(8,128)S(1)}, s32[]{:T(128)}, /*in...) while((s32[]{:T(128)}, f32[1,64,4,144]{3,1,2,0:T(8,128)S(1)}, ...), condition=%wide.region_3.4_spmd.clone.clone, body=%wide.region_1.3_spmd.sunk.clone.clone.sunk | while | flops 113545368 | bytes 1739467 | solution.py:155
  91.9 7.8 %collective-permute-done = f32[1,64,4,144]{3,1,2,0:T(8,128)S(1)} collective-permute-done((f32[1,64,4,144]{3,1,2,0:T(8,128)S(1)}, f32[1,64,4,144]{3,1,2,0:T(8,128)S(1)}, u32[]{:S(2)}, u32[]{:S(2)}) %collective-permute-start) | collective-permute-done | bytes 147488 | tf_op jit(solution)/shard_map/while/body/eval_jaxpr/ppermute | solution.py:39
  103.6 8.4 %collective-permute-done = f32[1,64,4,144]{3,1,2,0:T(8,128)S(1)} collective-permute-done((f32[1,64,4,144]{3,1,2,0:T(8,128)S(1)}, f32[1,64,4,144]{3,1,2,0:T(8,128)S(1)}, u32[]{:S(2)}, u32[]{:S(2)}) %collective-permute-start) | collective-permute-done | bytes 147488 | tf_op jit(solution)/shard_map/while/body/eval_jaxpr/ppermute | solution.py:39
  116.0 8.4 %collective-permute-done = f32[1,64,4,144]{3,1,2,0:T(8,128)S(1)} collective-permute-done((f32[1,64,4,144]{3,1,2,0:T(8,128)S(1)}, f32[1,64,4,144]{3,1,2,0:T(8,128)S(1)}, u32[]{:S(2)}, u32[]{:S(2)}) %collective-permute-start) | collective-permute-done | bytes 147488 | tf_op jit(solution)/shard_map/while/body/eval_jaxpr/ppermute | solution.py:39
  128.3 8.4 %collective-permute-done = f32[1,64,4,144]{3,1,2,0:T(8,128)S(1)} collective-permute-done((f32[1,64,4,144]{3,1,2,0:T(8,128)S(1)}, f32[1,64,4,144]{3,1,2,0:T(8,128)S(1)}, u32[]{:S(2)}, u32[]{:S(2)}) %collective-permute-start) | collective-permute-done | bytes 147488 | tf_op jit(solution)/shard_map/while/body/eval_jaxpr/ppermute | solution.py:39
  140.7 8.4 %collective-permute-done = f32[1,64,4,144]{3,1,2,0:T(8,128)S(1)} collective-permute-done((f32[1,64,4,144]{3,1,2,0:T(8,128)S(1)}, f32[1,64,4,144]{3,1,2,0:T(8,128)S(1)}, u32[]{:S(2)}, u32[]{:S(2)}) %collective-permute-start) | collective-permute-done | bytes 147488 | tf_op jit(solution)/shard_map/while/body/eval_jaxpr/ppermute | solution.py:39
  153.0 9.1 %collective-permute-done = f32[1,64,4,144]{3,1,2,0:T(8,128)S(1)} collective-permute-done((f32[1,64,4,144]{3,1,2,0:T(8,128)S(1)}, f32[1,64,4,144]{3,1,2,0:T(8,128)S(1)}, u32[]{:S(2)}, u32[]{:S(2)}) %collective-permute-start) | collective-permute-done | bytes 147488 | tf_op jit(solution)/shard_map/while/body/eval_jaxpr/ppermute | solution.py:39
  166.1 10.3 %collective-permute-done = f32[1,64,4,144]{3,1,2,0:T(8,128)S(1)} collective-permute-done((f32[1,64,4,144]{3,1,2,0:T(8,128)S(1)}, f32[1,64,4,144]{3,1,2,0:T(8,128)S(1)}, u32[]{:S(2)}, u32[]{:S(2)}) %collective-permute-start) | collective-permute-done | bytes 147488 | tf_op jit(solution)/shard_map/while/body/eval_jaxpr/ppermute | solution.py:39
  180.2 11.1 %collective-permute-done = f32[1,64,4,144]{3,1,2,0:T(8,128)S(1)} collective-permute-done((f32[1,64,4,144]{3,1,2,0:T(8,128)S(1)}, f32[1,64,4,144]{3,1,2,0:T(8,128)S(1)}, u32[]{:S(2)}, u32[]{:S(2)}) %collective-permute-start) | collective-permute-done | bytes 147488 | tf_op jit(solution)/shard_map/while/body/eval_jaxpr/ppermute | solution.py:39
  195.2 10.2 %collective-permute-done = f32[1,64,4,144]{3,1,2,0:T(8,128)S(1)} collective-permute-done((f32[1,64,4,144]{3,1,2,0:T(8,128)S(1)}, f32[1,64,4,144]{3,1,2,0:T(8,128)S(1)}, u32[]{:S(2)}, u32[]{:S(2)}) %collective-permute-start) | collective-permute-done | bytes 147488 | tf_op jit(solution)/shard_map/while/body/eval_jaxpr/ppermute | solution.py:39
  209.3 9.4 %collective-permute-done = f32[1,64,4,144]{3,1,2,0:T(8,128)S(1)} collective-permute-done((f32[1,64,4,144]{3,1,2,0:T(8,128)S(1)}, f32[1,64,4,144]{3,1,2,0:T(8,128)S(1)}, u32[]{:S(2)}, u32[]{:S(2)}) %collective-permute-start) | collective-permute-done | bytes 147488 | tf_op jit(solution)/shard_map/while/body/eval_jaxpr/ppermute | solution.py:39
  222.6 8.5 %collective-permute-done = f32[1,64,4,144]{3,1,2,0:T(8,128)S(1)} collective-permute-done((f32[1,64,4,144]{3,1,2,0:T(8,128)S(1)}, f32[1,64,4,144]{3,1,2,0:T(8,128)S(1)}, u32[]{:S(2)}, u32[]{:S(2)}) %collective-permute-start) | collective-permute-done | bytes 147488 | tf_op jit(solution)/shard_map/while/body/eval_jaxpr/ppermute | solution.py:39
  235.0 8.4 %collective-permute-done = f32[1,64,4,144]{3,1,2,0:T(8,128)S(1)} collective-permute-done((f32[1,64,4,144]{3,1,2,0:T(8,128)S(1)}, f32[1,64,4,144]{3,1,2,0:T(8,128)S(1)}, u32[]{:S(2)}, u32[]{:S(2)}) %collective-permute-start) | collective-permute-done | bytes 147488 | tf_op jit(solution)/shard_map/while/body/eval_jaxpr/ppermute | solution.py:39
  247.4 8.4 %collective-permute-done = f32[1,64,4,144]{3,1,2,0:T(8,128)S(1)} collective-permute-done((f32[1,64,4,144]{3,1,2,0:T(8,128)S(1)}, f32[1,64,4,144]{3,1,2,0:T(8,128)S(1)}, u32[]{:S(2)}, u32[]{:S(2)}) %collective-permute-start) | collective-permute-done | bytes 147488 | tf_op jit(solution)/shard_map/while/body/eval_jaxpr/ppermute | solution.py:39
  259.7 8.4 %collective-permute-done = f32[1,64,4,144]{3,1,2,0:T(8,128)S(1)} collective-permute-done((f32[1,64,4,144]{3,1,2,0:T(8,128)S(1)}, f32[1,64,4,144]{3,1,2,0:T(8,128)S(1)}, u32[]{:S(2)}, u32[]{:S(2)}) %collective-permute-start) | collective-permute-done | bytes 147488 | tf_op jit(solution)/shard_map/while/body/eval_jaxpr/ppermute | solution.py:39
  272.1 8.4 %collective-permute-done = f32[1,64,4,144]{3,1,2,0:T(8,128)S(1)} collective-permute-done((f32[1,64,4,144]{3,1,2,0:T(8,128)S(1)}, f32[1,64,4,144]{3,1,2,0:T(8,128)S(1)}, u32[]{:S(2)}, u32[]{:S(2)}) %collective-permute-start) | collective-permute-done | bytes 147488 | tf_op jit(solution)/shard_map/while/body/eval_jaxpr/ppermute | solution.py:39
  (204 shorter events, 90.2 us)
Async XLA Ops:
  2.7 3.4 %copy-start.3 = (bf16[1,1,2,768,768]{4,3,2,1,0:T(8,128)(2,1)S(1)}, bf16[1,1,2,768,768]{4,3,2,1,0:T(8,128)(2,1)}, u32[]{:S(2)}) copy-start(bf16[1,1,2,768,768]{4,3,2,1,0:T(8,128)(2,1)} %param.11) | copy-start | bytes 7077892
  2.7 3.4 %copy-start.7 = (bf16[768,768]{1,0:T(8,128)(2,1)S(1)}, bf16[768,768]{1,0:T(8,128)(2,1)}, u32[]{:S(2)}) copy-start(bf16[768,768]{1,0:T(8,128)(2,1)} %select_n.123) | copy-start | bytes 3538948
  8.9 4.0 %copy-start.4 = (bf16[1,1,2,768,768]{4,3,2,1,0:T(8,128)(2,1)S(1)}, bf16[1,1,2,768,768]{4,3,2,1,0:T(8,128)(2,1)}, u32[]{:S(2)}) copy-start(bf16[1,1,2,768,768]{4,3,2,1,0:T(8,128)(2,1)} %param.11) | copy-start | bytes 7077892
  8.9 4.0 %copy-start.16 = (f32[768,768]{0,1:T(8,128)S(1)}, f32[768,768]{0,1:T(8,128)}, u32[]{:S(2)}) copy-start(f32[768,768]{0,1:T(8,128)} %fusion.27) | copy-start | bytes 7077892
  42.7 28.4 %copy-start.9 = (f32[1,4,12,12]{3,1,2,0:T(4,128)S(1)}, f32[1,4,12,12]{3,1,2,0:T(4,128)}, u32[]{:S(2)}) copy-start(f32[1,4,12,12]{3,1,2,0:T(4,128)} %param.18) | copy-start | bytes 6916
  47.9 23.6 %copy-start.14 = (s32[6]{0:T(128)S(1)}, s32[6]{0:T(128)}, u32[]{:S(2)}) copy-start(s32[6]{0:T(128)} %param.16) | copy-start | bytes 76
  47.9 23.6 %copy-start.15 = (s32[1,4]{1,0:T(1,128)S(1)}, s32[1,4]{1,0:T(1,128)}, u32[]{:S(2)}) copy-start(s32[1,4]{1,0:T(1,128)} %param.15) | copy-start | bytes 52
  47.9 23.9 %copy-start.12 = (f32[16,6]{0,1:T(8,128)S(1)}, f32[16,6]{0,1:T(8,128)}, u32[]{:S(2)}) copy-start(f32[16,6]{0,1:T(8,128)} %param.17) | copy-start | bytes 1156
  47.9 38.6 %all-to-all-start.1 = ((bf16[32,2,1,1,4,576]{5,4,1,3,2,0:T(4,128)(2,1)}), bf16[32,2,1,1,4,576]{5,4,1,3,2,0:T(4,128)(2,1)S(1)}, u32[]{:S(2)}, u32[]{:S(2)}) async-start(bf16[32,2,1,1,4,576]{5,4,1,3,2,0:T(4,128)(2,1)} %copy.57), calls=%async_computation.1 | async-start | bytes 655360 | tf_op jit(solution)/shard_map/all_to_all | solution.py:26
  89.4 10.4 %collective-permute-start = (f32[1,64,4,144]{3,1,2,0:T(8,128)S(1)}, f32[1,64,4,144]{3,1,2,0:T(8,128)S(1)}, u32[]{:S(2)}, u32[]{:S(2)}) collective-permute-start(f32[1,64,4,144]{3,1,2,0:T(8,128)S(1)} %fusion.88), channel_id=1, source_target_pairs={{960,0},{0,64},{64,128},{128,192},{192,256},{256,320},{320,384},{3... | collective-permute-start | bytes 442376 | tf_op jit(solution)/shard_map/while/body/eval_jaxpr/ppermute | solution.py:39
  101.7 10.4 %collective-permute-start = (f32[1,64,4,144]{3,1,2,0:T(8,128)S(1)}, f32[1,64,4,144]{3,1,2,0:T(8,128)S(1)}, u32[]{:S(2)}, u32[]{:S(2)}) collective-permute-start(f32[1,64,4,144]{3,1,2,0:T(8,128)S(1)} %fusion.88), channel_id=1, source_target_pairs={{960,0},{0,64},{64,128},{128,192},{192,256},{256,320},{320,384},{3... | collective-permute-start | bytes 442376 | tf_op jit(solution)/shard_map/while/body/eval_jaxpr/ppermute | solution.py:39
  114.1 10.4 %collective-permute-start = (f32[1,64,4,144]{3,1,2,0:T(8,128)S(1)}, f32[1,64,4,144]{3,1,2,0:T(8,128)S(1)}, u32[]{:S(2)}, u32[]{:S(2)}) collective-permute-start(f32[1,64,4,144]{3,1,2,0:T(8,128)S(1)} %fusion.88), channel_id=1, source_target_pairs={{960,0},{0,64},{64,128},{128,192},{192,256},{256,320},{320,384},{3... | collective-permute-start | bytes 442376 | tf_op jit(solution)/shard_map/while/body/eval_jaxpr/ppermute | solution.py:39
  126.4 10.4 %collective-permute-start = (f32[1,64,4,144]{3,1,2,0:T(8,128)S(1)}, f32[1,64,4,144]{3,1,2,0:T(8,128)S(1)}, u32[]{:S(2)}, u32[]{:S(2)}) collective-permute-start(f32[1,64,4,144]{3,1,2,0:T(8,128)S(1)} %fusion.88), channel_id=1, source_target_pairs={{960,0},{0,64},{64,128},{128,192},{192,256},{256,320},{320,384},{3... | collective-permute-start | bytes 442376 | tf_op jit(solution)/shard_map/while/body/eval_jaxpr/ppermute | solution.py:39
  138.7 10.4 %collective-permute-start = (f32[1,64,4,144]{3,1,2,0:T(8,128)S(1)}, f32[1,64,4,144]{3,1,2,0:T(8,128)S(1)}, u32[]{:S(2)}, u32[]{:S(2)}) collective-permute-start(f32[1,64,4,144]{3,1,2,0:T(8,128)S(1)} %fusion.88), channel_id=1, source_target_pairs={{960,0},{0,64},{64,128},{128,192},{192,256},{256,320},{320,384},{3... | collective-permute-start | bytes 442376 | tf_op jit(solution)/shard_map/while/body/eval_jaxpr/ppermute | solution.py:39
  151.1 11.1 %collective-permute-start = (f32[1,64,4,144]{3,1,2,0:T(8,128)S(1)}, f32[1,64,4,144]{3,1,2,0:T(8,128)S(1)}, u32[]{:S(2)}, u32[]{:S(2)}) collective-permute-start(f32[1,64,4,144]{3,1,2,0:T(8,128)S(1)} %fusion.88), channel_id=1, source_target_pairs={{960,0},{0,64},{64,128},{128,192},{192,256},{256,320},{320,384},{3... | collective-permute-start | bytes 442376 | tf_op jit(solution)/shard_map/while/body/eval_jaxpr/ppermute | solution.py:39
  164.1 12.2 %collective-permute-start = (f32[1,64,4,144]{3,1,2,0:T(8,128)S(1)}, f32[1,64,4,144]{3,1,2,0:T(8,128)S(1)}, u32[]{:S(2)}, u32[]{:S(2)}) collective-permute-start(f32[1,64,4,144]{3,1,2,0:T(8,128)S(1)} %fusion.88), channel_id=1, source_target_pairs={{960,0},{0,64},{64,128},{128,192},{192,256},{256,320},{320,384},{3... | collective-permute-start | bytes 442376 | tf_op jit(solution)/shard_map/while/body/eval_jaxpr/ppermute | solution.py:39
  178.3 13.0 %collective-permute-start = (f32[1,64,4,144]{3,1,2,0:T(8,128)S(1)}, f32[1,64,4,144]{3,1,2,0:T(8,128)S(1)}, u32[]{:S(2)}, u32[]{:S(2)}) collective-permute-start(f32[1,64,4,144]{3,1,2,0:T(8,128)S(1)} %fusion.88), channel_id=1, source_target_pairs={{960,0},{0,64},{64,128},{128,192},{192,256},{256,320},{320,384},{3... | collective-permute-start | bytes 442376 | tf_op jit(solution)/shard_map/while/body/eval_jaxpr/ppermute | solution.py:39
  193.3 12.2 %collective-permute-start = (f32[1,64,4,144]{3,1,2,0:T(8,128)S(1)}, f32[1,64,4,144]{3,1,2,0:T(8,128)S(1)}, u32[]{:S(2)}, u32[]{:S(2)}) collective-permute-start(f32[1,64,4,144]{3,1,2,0:T(8,128)S(1)} %fusion.88), channel_id=1, source_target_pairs={{960,0},{0,64},{64,128},{128,192},{192,256},{256,320},{320,384},{3... | collective-permute-start | bytes 442376 | tf_op jit(solution)/shard_map/while/body/eval_jaxpr/ppermute | solution.py:39
  207.4 11.3 %collective-permute-start = (f32[1,64,4,144]{3,1,2,0:T(8,128)S(1)}, f32[1,64,4,144]{3,1,2,0:T(8,128)S(1)}, u32[]{:S(2)}, u32[]{:S(2)}) collective-permute-start(f32[1,64,4,144]{3,1,2,0:T(8,128)S(1)} %fusion.88), channel_id=1, source_target_pairs={{960,0},{0,64},{64,128},{128,192},{192,256},{256,320},{320,384},{3... | collective-permute-start | bytes 442376 | tf_op jit(solution)/shard_map/while/body/eval_jaxpr/ppermute | solution.py:39
  220.7 10.4 %collective-permute-start = (f32[1,64,4,144]{3,1,2,0:T(8,128)S(1)}, f32[1,64,4,144]{3,1,2,0:T(8,128)S(1)}, u32[]{:S(2)}, u32[]{:S(2)}) collective-permute-start(f32[1,64,4,144]{3,1,2,0:T(8,128)S(1)} %fusion.88), channel_id=1, source_target_pairs={{960,0},{0,64},{64,128},{128,192},{192,256},{256,320},{320,384},{3... | collective-permute-start | bytes 442376 | tf_op jit(solution)/shard_map/while/body/eval_jaxpr/ppermute | solution.py:39
  233.1 10.4 %collective-permute-start = (f32[1,64,4,144]{3,1,2,0:T(8,128)S(1)}, f32[1,64,4,144]{3,1,2,0:T(8,128)S(1)}, u32[]{:S(2)}, u32[]{:S(2)}) collective-permute-start(f32[1,64,4,144]{3,1,2,0:T(8,128)S(1)} %fusion.88), channel_id=1, source_target_pairs={{960,0},{0,64},{64,128},{128,192},{192,256},{256,320},{320,384},{3... | collective-permute-start | bytes 442376 | tf_op jit(solution)/shard_map/while/body/eval_jaxpr/ppermute | solution.py:39
  245.4 10.4 %collective-permute-start = (f32[1,64,4,144]{3,1,2,0:T(8,128)S(1)}, f32[1,64,4,144]{3,1,2,0:T(8,128)S(1)}, u32[]{:S(2)}, u32[]{:S(2)}) collective-permute-start(f32[1,64,4,144]{3,1,2,0:T(8,128)S(1)} %fusion.88), channel_id=1, source_target_pairs={{960,0},{0,64},{64,128},{128,192},{192,256},{256,320},{320,384},{3... | collective-permute-start | bytes 442376 | tf_op jit(solution)/shard_map/while/body/eval_jaxpr/ppermute | solution.py:39
  257.8 10.4 %collective-permute-start = (f32[1,64,4,144]{3,1,2,0:T(8,128)S(1)}, f32[1,64,4,144]{3,1,2,0:T(8,128)S(1)}, u32[]{:S(2)}, u32[]{:S(2)}) collective-permute-start(f32[1,64,4,144]{3,1,2,0:T(8,128)S(1)} %fusion.88), channel_id=1, source_target_pairs={{960,0},{0,64},{64,128},{128,192},{192,256},{256,320},{320,384},{3... | collective-permute-start | bytes 442376 | tf_op jit(solution)/shard_map/while/body/eval_jaxpr/ppermute | solution.py:39
  270.1 10.4 %collective-permute-start = (f32[1,64,4,144]{3,1,2,0:T(8,128)S(1)}, f32[1,64,4,144]{3,1,2,0:T(8,128)S(1)}, u32[]{:S(2)}, u32[]{:S(2)}) collective-permute-start(f32[1,64,4,144]{3,1,2,0:T(8,128)S(1)} %fusion.88), channel_id=1, source_target_pairs={{960,0},{0,64},{64,128},{128,192},{192,256},{256,320},{320,384},{3... | collective-permute-start | bytes 442376 | tf_op jit(solution)/shard_map/while/body/eval_jaxpr/ppermute | solution.py:39
  (9 other events, 16.9 us)
where the time goes:
time: 283 us; the launch traced here: 282 us
  waiting for transfers between devices  145 us (51%)
  starting transfers between devices  52.5 us (19%)
  matrix products  33.7 us (12%)
  local copies, waits for them, and re-layouts  25.3 us (9%)
  other arithmetic  19.9 us (7%)
  blocking collectives  4 us (1%)
    ppermute x15, waiting for transfers between devices, from_behind(): return lax.ppermute(block, axis, route)  134 us
    ppermute x15, starting transfers between devices, from_behind(): return lax.ppermute(block, axis, route)  29.4 us
    all_to_all x1, starting transfers between devices, turned_blocks(): lax.all_to_all(blocks, axes[k], split_axis=k, concat_axis=k, tiled=True)  23.1 us
    dot_general x16, matrix products, weighted(): jnp.einsum('amcef,amfcx->aecx', mixing, imaged, precision=lax.Precision.H...  14.3 us
    dot_general x4, matrix products, dense_product(): jnp.einsum('erq,eqk->erk', former, latter, preferred_element_type=jnp.flo...  13.1 us
    all_to_all x1, waiting for transfers between devices, turned_blocks(): lax.all_to_all(blocks, axes[k], split_axis=k, concat_axis=k, tiled=True)  11.5 us
    mul x31, other arithmetic, weighted(): bond_live[:, :, None] * (occupied[:, :, None] + greater[None, None, :])  11 us
    another operation x5, local copies, waits for them, and re-layouts  11 us
  transfers between devices with their start and end apart: 16, of which 16 were waited for; matrix products, arithmetic and copies ran while one was open for 1% of the time, Pallas kernels for 0%

commit v1 on v0

v1 whole, which is shorter than its diff:
```python
import functools

import jax
import jax.numpy as jnp
from jax import lax
from jax.experimental import pallas as pl
from jax.experimental.pallas import tpu as pltpu
from jax.sharding import PartitionSpec as P

F32, BF16, I32 = jnp.float32, jnp.bfloat16, jnp.int32
NO, NX, ATOMS, ROWS, ORD = 12, 144, 64, 256, 768
HALF, SUB, WIN = 384, 192, 256


def iota(shape, dim):
    return lax.broadcasted_iota(I32, shape, dim)


def one(mask):
    return jnp.where(mask, 1.0, 0.0).astype(BF16)


def dot(a, b):
    return lax.dot_general(a, b, (((1,), (0,)), ((), ())), preferred_element_type=F32)


def dot_t(a, b):
    return lax.dot_general(a, b, (((1,), (1,)), ((), ())), preferred_element_type=F32)


def pick_lanes(parts):
    lane = iota((ROWS, 128), 1)
    tiles = [parts[0][:, :128]]
    for t in range(1, 4):
        tiles.append(jnp.where(lane < 16 * t, parts[t - 1][:, 128:], parts[t][:, :128]))
    tiles.append(parts[3][:, 128:])
    return tiles


def blocks_kernel(nb_ref, g_ref, s_ref, out_ref, z_ref):
    spread = one(iota((HALF, NO), 0) % NO == iota((HALF, NO), 1))
    same = iota((HALF, ORD), 0) // NO == (iota((HALF, ORD), 1) % HALF) // NO
    left, right_r, right_i = [], [], []
    for t in range(2):
        cols = slice(HALF * t, HALF * (t + 1))
        g_r, g_i = g_ref[0, :, cols], g_ref[1, :, cols]
        s_r, s_i = s_ref[0, :, cols], s_ref[1, :, cols]
        upper = dot(spread, jnp.concatenate([s_r, s_i], axis=1))
        lower = dot(spread, jnp.concatenate([-s_i, s_r], axis=1))
        factor = jnp.concatenate(
            [jnp.where(same, upper, 0.0).astype(BF16), jnp.where(same, lower, 0.0).astype(BF16)], axis=0
        )
        both = jnp.concatenate([g_r, g_i], axis=1)
        left.append(dot(both, factor).astype(BF16))
        right_r.append(both)
        right_i.append(jnp.concatenate([-g_i, g_r], axis=1))
    left = jnp.concatenate(left, axis=1)
    right_r = jnp.concatenate(right_r, axis=1)
    right_i = jnp.concatenate(right_i, axis=1)
    own = iota((SUB, NX), 1) // NO == iota((SUB, NX), 0) % NO
    for h in range(4):
        rows = slice(SUB * h, SUB * (h + 1))
        odd = h % 2
        base = HALF * (h // 2) + 128 * odd
        window = slice(base, base + WIN)
        block = slice(HALF * (h // 2), HALF * (h // 2 + 1))
        mine = left[rows]
        turn = one(iota((SUB, HALF), 1) == iota((SUB, HALF), 0) + SUB * odd)
        diagonal = (iota((SUB, WIN), 0) + SUB * odd) // NO == (iota((SUB, WIN), 1) + 128 * odd) // NO
        fold = one((iota((WIN, NX), 0) + 128 * odd) % NO == iota((WIN, NX), 1) % NO)
        for part, right, sign in ((0, right_r, -1.0), (1, right_i, 1.0)):
            lesser = dot_t(mine, right[window])
            plain = g_ref[part, rows, window].astype(F32)
            turned = dot_t(turn, g_ref[part, window, block])
            greater = lesser + (plain + sign * turned)
            for c, value in ((part, lesser), (2 + part, greater)):
                folded = dot(jnp.where(diagonal, value, 0.0).astype(BF16), fold)
                z_ref[c, rows, :] = jnp.where(own, folded, 0.0).astype(BF16)
    gather = one(iota((ATOMS, ORD), 1) // NO == iota((ATOMS, ORD), 0))
    blocks = jnp.concatenate([dot(gather, z_ref[c]).astype(BF16) for c in range(4)], axis=0)
    tiled = dot(blocks, one(iota((NX, 640), 1) % NX == iota((NX, 640), 0))).astype(BF16)
    column = iota((ROWS, ROWS), 1)
    row = iota((ROWS, ROWS), 0)
    parts = []
    for m in range(4):
        wanted = (row & 3) * ATOMS + nb_ref[:, m : m + 1]
        parts.append(dot(one(column == wanted), tiled[:, 128 * m : 128 * m + WIN]))
    tiles = pick_lanes(parts)
    packed = jnp.concatenate(tiles, axis=1)[:, : 4 * NX]
    out_ref[...] = packed.reshape(ATOMS, 4, 4 * NX).astype(BF16)


def image_kernel(shift_ref, live_ref, c_ref, p_ref, out_ref):
    rows, lanes = iota((4 * NX, 4 * NX), 0), iota((4 * NX, 4 * NX), 1)
    coupling = c_ref[...]
    factors = []
    for outer in (True, False):
        lane = iota((NO, 4 * NX), 1)
        wide = (lane % NX) // NO if outer else lane % NO
        spread = jnp.where(iota((NO, 4 * NX), 0) == wide, 1.0, 0.0)
        wide = lax.dot_general(
            coupling, spread, (((1,), (0,)), ((), ())), precision=lax.Precision.HIGHEST, preferred_element_type=F32
        )
        high = wide.astype(BF16)
        rest = wide - high.astype(F32)
        middle = rest.astype(BF16)
        low = (rest - middle.astype(F32)).astype(BF16)
        stacked = jnp.concatenate([high, middle, low], axis=0)
        row = iota((4 * NX, 3 * 48), 0)
        source = (row // NX) * NO + ((row % NX) // NO if outer else row % NO)
        factors.append(dot(one(iota((4 * NX, 3 * 48), 1) % 48 == source), stacked))
    kron = jnp.where(rows // NX == lanes // NX, factors[0] * factors[1], 0.0).astype(BF16)
    pieces = p_ref[...].astype(F32).reshape(ROWS, 4 * NX).astype(BF16)
    imaged = dot(pieces, kron).astype(BF16)
    imaged = jnp.concatenate([imaged, jnp.zeros((ROWS, 64), BF16)], axis=1)
    row, column = iota((ROWS, ROWS), 0), iota((ROWS, ROWS), 1)
    gap = column - row
    is_greater = (row & 2) > 0
    pairs, totals = [], []
    for m in range(4):
        step = 4 * shift_ref[m]
        window = imaged[:, 128 * m : 128 * m + WIN]
        lower, upper = gap == -step, gap == step
        weight = live_ref[m].astype(F32)
        both = jnp.where(lower | upper, weight, 0.0).astype(BF16)
        single = jnp.where(jnp.where(is_greater, -gap, gap) == step, weight, 0.0).astype(BF16)
        pairs.append(dot(both, window))
        totals.append(dot(single, window))
    tiles = pick_lanes(pairs)
    sums = jnp.concatenate(pick_lanes(totals), axis=1).astype(BF16)
    lane, target = iota((640, WIN), 0), iota((640, WIN), 1) - 64
    fold = one((lane < 4 * NX) & (target >= 0) & (target < NX) & (lane % NX == target))
    total = dot(sums, fold)
    last = jnp.where(iota((ROWS, 128), 1) < 64, tiles[4], total[:, :128])
    for t, tile in enumerate([*tiles[:4], last, total[:, 128:]]):
        out_ref[:, 128 * t : 128 * (t + 1)] = tile.astype(BF16)


def momentum_kernel(n_ref, v_ref, out_ref):
    row, lane = iota((16, ROWS), 0), iota((16, ROWS), 1)
    transfer = (row - lane // 16) & 15
    spread = one(iota((ROWS, 16), 0) // 16 == iota((ROWS, 16), 1))
    same = (iota((ROWS, ROWS), 0) & 15) == (iota((ROWS, ROWS), 1) & 15)
    acc = jnp.zeros((ROWS, NX), F32)
    for m in range(5):
        window = v_ref[:, 128 * m : 128 * m + WIN]
        move = one(iota((WIN, NX), 0) == iota((WIN, NX), 1) + 16 * m)
        pieces = dot(window, move).astype(BF16)
        if m == 4:
            acc += dot(jnp.where(same, 1.0 / 16, 0.0).astype(BF16), pieces)
            continue
        weights = jnp.zeros((16, ROWS), F32)
        for q in range(16):
            weights = jnp.where(transfer == q, n_ref[m, q] * (1.0 / 16), weights)
        high = weights.astype(BF16)
        low = (weights - high.astype(F32)).astype(BF16)
        for part in (high, low):
            acc += dot(jnp.where(same, dot(spread, part), 0.0).astype(BF16), pieces)
    out_ref[...] = acc.astype(BF16)


VMEM = pl.BlockSpec(memory_space=pltpu.VMEM)
SMEM = pl.BlockSpec(memory_space=pltpu.SMEM)


def call(kernel, out, specs, scratch=()):
    return pl.pallas_call(
        kernel,
        out_shape=jax.ShapeDtypeStruct(out, BF16),
        in_specs=specs,
        out_specs=VMEM,
        scratch_shapes=scratch,
        compiler_params=pltpu.CompilerParams(vmem_limit_bytes=48 << 20),
    )


def blocks_of(neighbours, retarded, injection):
    rows = jnp.repeat(neighbours, 4, axis=0)
    f = call(blocks_kernel, (ATOMS, 4, 4 * NX), [VMEM, VMEM, VMEM], [pltpu.VMEM((4, ORD, NX), BF16)])
    return f(rows, retarded, injection)


def image_of(shift, live, coupling, pieces):
    turned = jnp.swapaxes(coupling, 1, 2).reshape(4 * NO, NO)
    return call(image_kernel, (ROWS, ORD), [SMEM, SMEM, VMEM, VMEM])(shift, live, turned, pieces)


def convolved(occupied, pieces):
    return call(momentum_kernel, (ROWS, NX), [SMEM, VMEM])(occupied, pieces)


def exchange(x, axis):
    return lax.all_to_all(x, axis, split_axis=0, concat_axis=0, tiled=True)


def per_device(retarded, injection, neighbours, bond_count, bond_mode, mode_shift, occupation, coupling):
    shift = mode_shift[bond_mode[0]]
    live = (jnp.arange(4, dtype=I32) < bond_count[0]).astype(I32)
    occupied = occupation.T[bond_mode[0]]
    sent = blocks_of(neighbours, retarded[0, 0], injection[0, 0])
    pieces = exchange(sent, "en")
    imaged = image_of(shift, live, coupling[0], pieces)
    spread = exchange(imaged.reshape(16, 16, ORD), "mom")
    scattered = convolved(occupied, spread.reshape(ROWS, ORD))
    back = exchange(scattered.reshape(16, 16, NX), "mom")
    return back.reshape(1, 1, ATOMS, 4, NX).astype(F32)


def solution(mesh):
    en = P("en")
    in_specs = (
        P("mom", "en", None, None, None),
        P("mom", "en", None, None, None),
        P(),
        en,
        P("en", None),
        P(),
        P(),
        P("en", None, None, None),
    )
    return jax.shard_map(
        per_device,
        mesh=mesh,
        in_specs=in_specs,
        out_specs=P("mom", "en", None, None, None),
        check_vma=False,
    )
```

time: 283 us -> 91.9 us (0.32)
  the two profiles are of different devices: /device:TPU:8 before, /device:TPU:1 now
where the time goes in v1:
time: 91.9 us; the launch traced here: 91.4 us
  starting transfers between devices  31 us (34%)
  waiting for transfers between devices  28 us (30%)
  Pallas kernels  13.8 us (15%)
  blocking collectives  12.4 us (13%)
  local copies, waits for them, and re-layouts  5.44 us (6%)
    all_to_all x2, starting transfers between devices, exchange(): return lax.all_to_all(x, axis, split_axis=0, concat_axis=0, tiled=True)  31 us
    all_to_all x2, waiting for transfers between devices, exchange(): return lax.all_to_all(x, axis, split_axis=0, concat_axis=0, tiled=True)  28 us
    all_to_all x1, blocking collectives, exchange(): return lax.all_to_all(x, axis, split_axis=0, concat_axis=0, tiled=True)  12.4 us
    pallas_call x1, Pallas kernels, blocks_of(): return f(rows, retarded, injection)  8.61 us
    pallas_call x1, Pallas kernels, image_of(): call(image_kernel, (ROWS, ORD), [SMEM, SMEM, VMEM, VMEM])  3.41 us
    unnamed x12, local copies, waits for them, and re-layouts  3.26 us
  transfers between devices with their start and end apart: 2, of which 2 were waited for; matrix products, arithmetic and copies ran while one was open for 2% of the time, Pallas kernels for 0%

profile of v1, /device:TPU:1, one launch (start us, length us, event | category | flops | bytes accessed | tf_op | source)
XLA Modules:
  0.0 91.4 jit_solution(18039423776376537104)
XLA Ops:
  0.0 0.0 copy-start
  0.0 0.0 copy-start.3
  0.0 0.0 copy-start.2
  0.0 0.8 copy.12
  0.8 0.8 copy.16
  1.6 0.0 copy-start.1
  1.6 1.7 %copy-done.1 = bf16[1,1,2,768,768]{4,3,2,1,0:T(8,128)(2,1)S(1)} copy-done((bf16[1,1,2,768,768]{4,3,2,1,0:T(8,128)(2,1)S(1)}, bf16[1,1,2,768,768]{4,3,2,1,0:T(8,128)(2,1)}, u32[]{:S(2)}) %copy-start.1) | copy-done | bytes 2359320
  3.3 8.6 %shard_map.82 = bf16[64,4,576]{2,1,0:T(4,128)(2,1)} custom-call(s32[256,4]{1,0:T(8,128)S(1)} %bitcast.23, bf16[2,768,768]{2,1,0:T(8,128)(2,1)S(1)} %bitcast.21, bf16[2,12,768]{2,1,0:T(8,128)(2,1)S(1)} %bitcast.25), custom_call_target="tpu_custom_call" | custom-call | tf_op jit(solution)/shard_map/pallas_call | solution.py:180
  11.9 24.4 %all-to-all-start = ((bf16[64,4,576]{2,1,0:T(4,128)(2,1)}), bf16[64,4,576]{2,1,0:T(4,128)(2,1)S(1)}, u32[]{:S(2)}, u32[]{:S(2)}) async-start(bf16[64,4,576]{2,1,0:T(4,128)(2,1)} %shard_map.82), calls=%async_computation | async-start | bytes 655360 | tf_op jit(solution)/shard_map/all_to_all | solution.py:193
  37.0 0.0 copy-done.3
  37.0 0.1 reshape.58
  37.1 0.1 copy.14.c_ref
  37.2 0.0 copy-done.4
  37.2 0.0 copy-done.2
  37.2 0.6 gather_fusion.1
  37.9 15.1 %all-to-all-done.p_ref = bf16[64,4,576]{2,1,0:T(4,128)(2,1)S(1)} async-done(((bf16[64,4,576]{2,1,0:T(4,128)(2,1)}), bf16[64,4,576]{2,1,0:T(4,128)(2,1)S(1)}, u32[]{:S(2)}, u32[]{:S(2)}) %all-to-all-start) | async-done | bytes 294944 | tf_op jit(solution)/shard_map/all_to_all | solution.py:193
  53.0 3.4 %shard_map.83 = bf16[256,768]{1,0:T(8,128)(2,1)} custom-call(s32[4]{0:T(128)S(1)} %gather_fusion.1, s32[4]{0:T(128)S(1)} %compare_convert_fusion.live_ref, f32[48,12]{1,0:T(8,128)S(1)} %copy.14.c_ref, bf16[64,4,576]{2,1,0:T(4,128)(2,1)S(1)} %all-to-all-done.p_ref), custom_call_target="tpu_custom_call" | custom-call | tf_op jit(solution)/shard_map/pallas_call | solution.py:185
  56.4 6.6 %all-to-all-start.1 = ((bf16[16,16,768]{2,1,0:T(8,128)(2,1)}), bf16[16,16,768]{2,1,0:T(8,128)(2,1)S(1)}, u32[]{:S(2)}, u32[]{:S(2)}) async-start(bf16[16,16,768]{2,1,0:T(8,128)(2,1)} %bitcast.9), calls=%async_computation.1 | async-start | bytes 786432 | tf_op jit(solution)/shard_map/all_to_all | solution.py:193
  63.0 0.0 copy-done
  63.0 0.6 gather_fusion
  63.5 12.9 %all-to-all-done.1 = bf16[16,16,768]{2,1,0:T(8,128)(2,1)S(1)} async-done(((bf16[16,16,768]{2,1,0:T(8,128)(2,1)}), bf16[16,16,768]{2,1,0:T(8,128)(2,1)S(1)}, u32[]{:S(2)}, u32[]{:S(2)}) %all-to-all-start.1) | async-done | bytes 393248 | tf_op jit(solution)/shard_map/all_to_all | solution.py:193
  76.5 1.8 %shard_map.84 = bf16[256,144]{1,0:T(8,128)(2,1)S(1)} custom-call(f32[4,16]{1,0:T(4,128)S(1)} %gather_fusion, bf16[256,768]{1,0:T(8,128)(2,1)S(1)} %bitcast.22), custom_call_target="tpu_custom_call" | custom-call | tf_op jit(solution)/shard_map/pallas_call | solution.py:189
  78.2 12.4 %all_to_all.15 = bf16[16,16,144]{2,1,0:T(8,128)(2,1)S(1)} all-to-all(bf16[16,16,144]{2,1,0:T(8,128)(2,1)S(1)} %bitcast.24), channel_id=1, replica_groups=mesh['mom'=16,'en'=64] {'mom'}, dimensions={0} | all-to-all | bytes 147456 | tf_op jit(solution)/shard_map/all_to_all | solution.py:193
  90.7 0.8 reshape.63
  (5 shorter events, 0.0 us)
Async XLA Ops:
  0.0 63.0 %copy-start = (f32[16,6]{0,1:T(8,128)S(1)}, f32[16,6]{0,1:T(8,128)}, u32[]{:S(2)}) copy-start(f32[16,6]{0,1:T(8,128)} %param.14) | copy-start | bytes 1156
  0.0 37.0 %copy-start.3 = (f32[1,4,12,12]{3,1,2,0:T(4,128)S(1)}, f32[1,4,12,12]{3,1,2,0:T(4,128)}, u32[]{:S(2)}) copy-start(f32[1,4,12,12]{3,1,2,0:T(4,128)} %param.15) | copy-start | bytes 6916
  0.0 37.2 %copy-start.4 = (s32[1,4]{1,0:T(1,128)S(1)}, s32[1,4]{1,0:T(1,128)}, u32[]{:S(2)}) copy-start(s32[1,4]{1,0:T(1,128)} %param.12) | copy-start | bytes 52
  0.0 37.2 %copy-start.2 = (s32[6]{0:T(128)S(1)}, s32[6]{0:T(128)}, u32[]{:S(2)}) copy-start(s32[6]{0:T(128)} %param.13) | copy-start | bytes 76
  1.6 1.7 %copy-start.1 = (bf16[1,1,2,768,768]{4,3,2,1,0:T(8,128)(2,1)S(1)}, bf16[1,1,2,768,768]{4,3,2,1,0:T(8,128)(2,1)}, u32[]{:S(2)}) copy-start(bf16[1,1,2,768,768]{4,3,2,1,0:T(8,128)(2,1)} %param.8) | copy-start | bytes 7077892
  11.9 41.1 %all-to-all-start = ((bf16[64,4,576]{2,1,0:T(4,128)(2,1)}), bf16[64,4,576]{2,1,0:T(4,128)(2,1)S(1)}, u32[]{:S(2)}, u32[]{:S(2)}) async-start(bf16[64,4,576]{2,1,0:T(4,128)(2,1)} %shard_map.82), calls=%async_computation | async-start | bytes 655360 | tf_op jit(solution)/shard_map/all_to_all | solution.py:193
  56.4 20.1 %all-to-all-start.1 = ((bf16[16,16,768]{2,1,0:T(8,128)(2,1)}), bf16[16,16,768]{2,1,0:T(8,128)(2,1)S(1)}, u32[]{:S(2)}, u32[]{:S(2)}) async-start(bf16[16,16,768]{2,1,0:T(8,128)(2,1)} %bitcast.9), calls=%async_computation.1 | async-start | bytes 786432 | tf_op jit(solution)/shard_map/all_to_all | solution.py:193

commit v2 on v1

v2 whole, which is shorter than its diff:
```python
import functools

import jax
import jax.numpy as jnp
from jax import lax
from jax.experimental import pallas as pl
from jax.experimental.pallas import tpu as pltpu
from jax.sharding import PartitionSpec as P

F32, BF16, I32 = jnp.float32, jnp.bfloat16, jnp.int32
NO, NX, ATOMS, ROWS, ORD = 12, 144, 64, 256, 768
HALF, SUB, WIN = 384, 192, 256


def iota(shape, dim):
    return lax.broadcasted_iota(I32, shape, dim)


def one(mask):
    return jnp.where(mask, 1.0, 0.0).astype(BF16)


def dot(a, b):
    return lax.dot_general(a, b, (((1,), (0,)), ((), ())), preferred_element_type=F32)


def dot_t(a, b):
    return lax.dot_general(a, b, (((1,), (1,)), ((), ())), preferred_element_type=F32)


def pick_lanes(parts):
    lane = iota((ROWS, 128), 1)
    tiles = [parts[0][:, :128]]
    for t in range(1, 4):
        tiles.append(jnp.where(lane < 16 * t, parts[t - 1][:, 128:], parts[t][:, :128]))
    tiles.append(parts[3][:, 128:])
    return tiles


def blocks_kernel(nb_hbm, s_hbm, g_hbm, out_ref, nb_ref, s_ref, g_ref, left_ref, z_ref, sems):
    small = [pltpu.make_async_copy(s_hbm, s_ref, sems.at[4]), pltpu.make_async_copy(nb_hbm, nb_ref, sems.at[5])]
    for copy in small:
        copy.start()
    copies = []
    for t in range(2):
        for part in range(2):
            rows = pl.ds(HALF * t, HALF)
            copies.append(
                pltpu.make_async_copy(g_hbm.at[part, rows, :], g_ref.at[part, rows, :], sems.at[2 * t + part])
            )
    for copy in copies:
        copy.start()
    for copy in small:
        copy.wait()
    spread = one((iota((128, NO), 0) + 8) % NO == iota((128, NO), 1))
    s_r = s_ref[:, 0, :].astype(F32)
    s_i = s_ref[:, 1, :].astype(F32)
    tall, wide = iota((128, 128), 0), iota((128, 128), 1)
    factors = []
    for t in range(6):
        cols = slice(128 * t, 128 * (t + 1))
        both = jnp.concatenate([s_r[:, cols], s_i[:, cols]], axis=1).astype(BF16)
        for shifts in ((0, 0), (1, -1)):
            near = jnp.where(tall < 64, 128 * (t + shifts[0]), 128 * (t + shifts[1])) + tall
            orbital = jnp.where(
                iota((128, NO), 0) < 64, 128 * (t + shifts[0]) + 240, 128 * (t + shifts[1]) + 240
            ) + iota((128, NO), 0)
            pick = one(orbital % NO == iota((128, NO), 1))
            rows = dot(pick, both)
            same = (near + 240) // NO == (128 * t + wide + 240) // NO
            real = jnp.where(same, rows[:, :128], 0.0)
            imag = jnp.where(same, rows[:, 128:], 0.0)
            upper = jnp.concatenate([real, imag], axis=1)
            lower = jnp.concatenate([-imag, real], axis=1)
            factors.append(jnp.concatenate([upper, lower], axis=0).astype(BF16))
    lane = iota((HALF, 128), 1)
    own = iota((4 * SUB, NX), 1) // NO == iota((4 * SUB, NX), 0) % NO
    for half in range(2):
        rows = slice(HALF * half, HALF * (half + 1))
        copies[2 * half].wait()
        copies[2 * half + 1].wait()
        tiles = [[g_ref[part, rows, 128 * t : 128 * (t + 1)] for part in range(2)] for t in range(6)]
        for t in range(6):
            low, high = tiles[max(t - 1, 0)], tiles[min(t + 1, 5)]
            beside = [jnp.where(lane < 64, high[part], low[part]) for part in range(2)]
            line = dot(jnp.concatenate(tiles[t], axis=1), factors[2 * t])
            line += dot(jnp.concatenate(beside, axis=1), factors[2 * t + 1])
            line = line.astype(BF16)
            left_ref[0, :, 256 * t : 256 * t + 256] = line
            left_ref[1, :, 256 * t : 256 * t + 128] = line[:, 128:]
            left_ref[1, :, 256 * t + 128 : 256 * t + 256] = -line[:, :128]
        right = jnp.concatenate([piece for tile in tiles for piece in tile], axis=1)
        for odd in range(2):
            mine = slice(SUB * odd, SUB * (odd + 1))
            window = slice(128 * odd, 128 * odd + WIN)
            stacked = jnp.concatenate([left_ref[0, mine, :], left_ref[1, mine, :]], axis=0)
            lesser = dot_t(stacked, right[window])
            turn = one(iota((SUB, WIN), 1) + 128 * odd == iota((SUB, WIN), 0) + SUB * odd)
            base = HALF * half
            square = slice(base + 128 * odd, base + 128 * odd + WIN)
            values = [lesser[:SUB], lesser[SUB:]]
            for part, sign in ((0, -1.0), (1, 1.0)):
                plain = g_ref[part, base + SUB * odd : base + SUB * (odd + 1), square].astype(F32)
                turned = dot_t(turn, g_ref[part, square, square])
                values.append(values[part] + (plain + sign * turned))
            diagonal = (iota((SUB, WIN), 0) + SUB * odd) // NO == (iota((SUB, WIN), 1) + 128 * odd) // NO
            fold = one((iota((WIN, NX), 0) + 128 * odd) % NO == iota((WIN, NX), 1) % NO)
            kept = jnp.concatenate([jnp.where(diagonal, v, 0.0).astype(BF16) for v in values], axis=0)
            folded = jnp.where(own, dot(kept, fold), 0.0).astype(BF16)
            for c in range(4):
                z_ref[c, base + SUB * odd : base + SUB * (odd + 1), :] = folded[SUB * c : SUB * (c + 1)]
    gather = one(iota((ATOMS, ORD), 1) // NO == iota((ATOMS, ORD), 0))
    blocks = jnp.concatenate([dot(gather, z_ref[c]).astype(BF16) for c in range(4)], axis=0)
    tiled = dot(blocks, one(iota((NX, 640), 1) % NX == iota((NX, 640), 0))).astype(BF16)
    column, row = iota((ROWS, ROWS), 1), iota((ROWS, ROWS), 0)
    owner = one(iota((ROWS, ATOMS), 0) // 4 == iota((ROWS, ATOMS), 1))
    atoms = dot_t(owner, nb_ref[...].astype(F32).astype(BF16)).astype(I32)
    parts = []
    for m in range(4):
        wanted = (row & 3) * ATOMS + atoms[:, m : m + 1]
        parts.append(dot(one(column == wanted), tiled[:, 128 * m : 128 * m + WIN]))
    packed = jnp.concatenate(pick_lanes(parts), axis=1)[:, : 4 * NX]
    out_ref[...] = packed.reshape(ATOMS, 4, 4 * NX).astype(BF16)


def prepare_kernel(mode_ref, n_ref, c_ref, kron_ref, weight_ref):
    rows, lanes = iota((4 * NX, 4 * NX), 0), iota((4 * NX, 4 * NX), 1)
    coupling = jnp.concatenate([c_ref[m].T for m in range(4)], axis=0)
    factors = []
    for outer in (True, False):
        lane = iota((NO, 4 * NX), 1)
        wide = (lane % NX) // NO if outer else lane % NO
        spread = jnp.where(iota((NO, 4 * NX), 0) == wide, 1.0, 0.0)
        wide = lax.dot_general(
            coupling, spread, (((1,), (0,)), ((), ())), precision=lax.Precision.HIGHEST, preferred_element_type=F32
        )
        high = wide.astype(BF16)
        rest = wide - high.astype(F32)
        middle = rest.astype(BF16)
        low = (rest - middle.astype(F32)).astype(BF16)
        stacked = jnp.concatenate([high, middle, low], axis=0)
        row = iota((4 * NX, 3 * 48), 0)
        source = (row // NX) * NO + ((row % NX) // NO if outer else row % NO)
        factors.append(dot(one(iota((4 * NX, 3 * 48), 1) % 48 == source), stacked))
    kron_ref[...] = jnp.where(rows // NX == lanes // NX, factors[0] * factors[1], 0.0).astype(BF16)
    row, lane = iota((16, ROWS), 0), iota((16, ROWS), 1)
    transfer = (row - lane // 16) & 15
    spread = one(iota((ROWS, 16), 0) // 16 == iota((ROWS, 16), 1))
    same = (iota((ROWS, ROWS), 0) & 15) == (iota((ROWS, ROWS), 1) & 15)
    for m in range(4):
        weights = jnp.zeros((16, ROWS), F32)
        for q in range(16):
            weights = jnp.where(transfer == q, n_ref[mode_ref[0, m], q] * (1.0 / 16), weights)
        high = weights.astype(BF16)
        low = (weights - high.astype(F32)).astype(BF16)
        for i, part in enumerate((high, low)):
            weight_ref[2 * m + i] = jnp.where(same, dot(spread, part), 0.0).astype(BF16)


def image_kernel(count_ref, mode_ref, shift_ref, kron_ref, p_ref, out_ref):
    pieces = p_ref[...].astype(F32).reshape(ROWS, 4 * NX).astype(BF16)
    imaged = dot(pieces, kron_ref[...]).astype(BF16)
    imaged = jnp.concatenate([imaged, jnp.zeros((ROWS, 64), BF16)], axis=1)
    row, column = iota((ROWS, ROWS), 0), iota((ROWS, ROWS), 1)
    gap = column - row
    facing = jnp.where((row & 2) > 0, -gap, gap)
    pairs, totals = [], []
    for m in range(4):
        step = jnp.where(m < count_ref[0], 4 * shift_ref[mode_ref[0, m]], 4 * ROWS)
        window = imaged[:, 128 * m : 128 * m + WIN]
        pairs.append(dot(one(jnp.abs(gap) == step), window))
        totals.append(dot(one(facing == step), window))
    tiles = pick_lanes(pairs)
    sums = jnp.concatenate(pick_lanes(totals), axis=1).astype(BF16)
    lane, target = iota((640, WIN), 0), iota((640, WIN), 1) - 64
    fold = one((lane < 4 * NX) & (target >= 0) & (target < NX) & (lane % NX == target))
    total = dot(sums, fold)
    last = jnp.where(iota((ROWS, 128), 1) < 64, tiles[4], total[:, :128])
    for t, tile in enumerate([*tiles[:4], last, total[:, 128:]]):
        out_ref[:, 128 * t : 128 * (t + 1)] = tile.astype(BF16)


def momentum_kernel(weight_ref, v_ref, out_ref):
    same = (iota((ROWS, ROWS), 0) & 15) == (iota((ROWS, ROWS), 1) & 15)
    acc = jnp.zeros((ROWS, NX), F32)
    for m in range(5):
        window = v_ref[:, 128 * m : 128 * m + WIN]
        move = one(iota((WIN, NX), 0) == iota((WIN, NX), 1) + 16 * m)
        pieces = dot(window, move).astype(BF16)
        if m == 4:
            acc += dot(jnp.where(same, 1.0 / 16, 0.0).astype(BF16), pieces)
        else:
            acc += dot(weight_ref[2 * m], pieces) + dot(weight_ref[2 * m + 1], pieces)
    out_ref[...] = acc.astype(BF16)


VMEM = pl.BlockSpec(memory_space=pltpu.VMEM)
SMEM = pl.BlockSpec(memory_space=pltpu.SMEM)
HBM = pl.BlockSpec(memory_space=pltpu.HBM)


def call(kernel, outs, specs, scratch=()):
    shapes = [jax.ShapeDtypeStruct(out, BF16) for out in outs]
    return pl.pallas_call(
        kernel,
        out_shape=shapes if len(outs) > 1 else shapes[0],
        in_specs=specs,
        out_specs=[VMEM] * len(outs) if len(outs) > 1 else VMEM,
        scratch_shapes=scratch,
        compiler_params=pltpu.CompilerParams(vmem_limit_bytes=48 << 20),
    )


def blocks_of(neighbours, retarded, injection):
    scratch = [
        pltpu.VMEM((4, ATOMS), I32),
        pltpu.VMEM((NO, 2, ORD), BF16),
        pltpu.VMEM((2, ORD, ORD), BF16),
        pltpu.VMEM((2, HALF, 2 * ORD), BF16),
        pltpu.VMEM((4, ORD, NX), BF16),
        pltpu.SemaphoreType.DMA((6,)),
    ]
    f = call(blocks_kernel, [(ATOMS, 4, 4 * NX)], [HBM, HBM, HBM], scratch)
    operands = (neighbours.T, jnp.swapaxes(injection, 0, 1), retarded)
    return f(*(pltpu.with_memory_space_constraint(x, pltpu.HBM) for x in operands))


def prepared(bond_mode, occupation, coupling):
    f = call(prepare_kernel, [(4 * NX, 4 * NX), (8, ROWS, ROWS)], [SMEM, SMEM, VMEM])
    return f(bond_mode, occupation.T, coupling)


def image_of(bond_count, bond_mode, mode_shift, kron, pieces):
    f = call(image_kernel, [(ROWS, ORD)], [SMEM, SMEM, SMEM, VMEM, VMEM])
    return f(bond_count, bond_mode, mode_shift, kron, pieces)


def convolved(weights, pieces):
    return call(momentum_kernel, [(ROWS, NX)], [VMEM, VMEM])(weights, pieces)


def exchange(x, axis):
    return lax.all_to_all(x, axis, split_axis=0, concat_axis=0, tiled=True)


def per_device(retarded, injection, neighbours, bond_count, bond_mode, mode_shift, occupation, coupling):
    sent = blocks_of(neighbours, retarded[0, 0], injection[0, 0])
    kron, weights = prepared(bond_mode, occupation, coupling[0])
    pieces = exchange(sent, "en")
    imaged = image_of(bond_count, bond_mode, mode_shift, kron, pieces)
    spread = exchange(imaged.reshape(16, 16, ORD), "mom")
    scattered = convolved(weights, spread.reshape(ROWS, ORD))
    back = exchange(scattered.reshape(16, 16, NX), "mom")
    return back.reshape(1, 1, ATOMS, 4, NX).astype(F32)


def solution(mesh):
    en = P("en")
    in_specs = (
        P("mom", "en", None, None, None),
        P("mom", "en", None, None, None),
        P(),
        en,
        P("en", None),
        P(),
        P(),
        P("en", None, None, None),
    )
    return jax.shard_map(
        per_device,
        mesh=mesh,
        in_specs=in_specs,
        out_specs=P("mom", "en", None, None, None),
        check_vma=False,
    )
```

time: 91.9 us -> 85.1 us (0.926)
  blocking collectives: 12.4 us -> 32.3 us
  waiting for transfers between devices: 28 us -> 13.6 us
  starting transfers between devices: 31 us -> 24.5 us
  local copies, waits for them, and re-layouts: 5.44 us -> 0.8 us
    all_to_all x1 -> x2, blocking collectives: 12.4 us -> 32.3 us  [exchange(): return lax.all_to_all(x, axis, split_axis=0, concat_axis=0, tiled=True)]
    all_to_all x2 -> x1, waiting for transfers between devices: 28 us -> 13.6 us  [exchange(): return lax.all_to_all(x, axis, split_axis=0, concat_axis=0, tiled=True)]
    all_to_all x2 -> x1, starting transfers between devices: 31 us -> 24.5 us  [exchange(): return lax.all_to_all(x, axis, split_axis=0, concat_axis=0, tiled=True)]
    unnamed x12 -> x9, local copies, waits for them, and re-layouts: 3.26 us -> 0.02 us
    gather x2 -> x0, local copies, waits for them, and re-layouts: 1.2 us -> none  [the longest x1 0.64 us: per_device(): shift = mode_shift[bond_mode[0]]]
    pallas_call x3 -> x4, Pallas kernels: 13.8 us -> 12.9 us  [the longest x1 7.93 us: blocks_of(): f(*(pltpu.with_memory_space_constraint(x, pltpu.HBM) for x in operands))]
  transfers between devices with their start and end apart: 2 -> 1, of which waited for: 2 -> 1; matrix products, arithmetic and copies ran while one was open for 2% -> 0% of each run, Pallas kernels for 0% -> 3%
where the time goes in v2:
time: 85.1 us; the launch traced here: 84.8 us
  blocking collectives  32.3 us (38%)
  starting transfers between devices  24.5 us (29%)
  waiting for transfers between devices  13.6 us (16%)
  Pallas kernels  12.9 us (15%)
    all_to_all x2, blocking collectives, exchange(): return lax.all_to_all(x, axis, split_axis=0, concat_axis=0, tiled=True)  32.3 us
    all_to_all x1, starting transfers between devices, exchange(): return lax.all_to_all(x, axis, split_axis=0, concat_axis=0, tiled=True)  24.5 us
    all_to_all x1, waiting for transfers between devices, exchange(): return lax.all_to_all(x, axis, split_axis=0, concat_axis=0, tiled=True)  13.6 us
    pallas_call x1, Pallas kernels, blocks_of(): f(*(pltpu.with_memory_space_constraint(x, pltpu.HBM) for x in operands))  7.93 us
    pallas_call x1, Pallas kernels, prepared(): return f(bond_mode, occupation.T, coupling)  2.27 us
  transfers between devices with their start and end apart: 1, of which 1 were waited for; matrix products, arithmetic and copies ran while one was open for 0% of the time, Pallas kernels for 3%

profile of v2, /device:TPU:1, one launch (start us, length us, event | category | flops | bytes accessed | tf_op | source)
XLA Modules:
  0.0 84.8 jit_solution(7275285709437419740)
XLA Ops:
  0.0 0.0 copy-start.3
  0.0 0.0 copy-start.1
  0.0 0.0 copy-start
  0.0 0.0 copy-start.2
  0.0 7.9 %shard_map.83 = bf16[64,4,576]{2,1,0:T(4,128)(2,1)} custom-call(s32[4,64]{1,0:T(4,128)} %bitcast.19, bf16[12,2,768]{2,1,0:T(2,128)(2,1)} %bitcast.18, bf16[2,768,768]{2,1,0:T(8,128)(2,1)} %bitcast.17), custom_call_target="tpu_custom_call" | custom-call | tf_op jit(solution)/shard_map/pallas_call | solution.py:225
  8.0 24.5 %all-to-all-start = ((bf16[64,4,576]{2,1,0:T(4,128)(2,1)}), bf16[64,4,576]{2,1,0:T(4,128)(2,1)S(1)}, u32[]{:S(2)}, u32[]{:S(2)}) async-start(bf16[64,4,576]{2,1,0:T(4,128)(2,1)} %shard_map.83), calls=%async_computation | async-start | bytes 655360 | tf_op jit(solution)/shard_map/all_to_all | solution.py:243
  33.1 0.0 copy-done.3
  33.1 0.0 copy-done.1
  33.1 0.0 copy-done
  33.1 2.3 %shard_map.82 = (bf16[576,576]{1,0:T(8,128)(2,1)S(1)}, bf16[8,256,256]{2,1,0:T(8,128)(2,1)S(1)}) custom-call(s32[1,4]{1,0:T(1,128)S(1)} %copy-done.1, f32[6,16]{1,0:T(8,128)S(1)} %bitcast.16, f32[4,12,12]{2,1,0:T(8,128)S(1)} %bitcast.15), custom_call_target="tpu_custom_call" | custom-call | tf_op jit(solution)/shard_map/pallas_call | solution.py:230
  35.4 13.6 %all-to-all-done.p_ref = bf16[64,4,576]{2,1,0:T(4,128)(2,1)S(1)} async-done(((bf16[64,4,576]{2,1,0:T(4,128)(2,1)}), bf16[64,4,576]{2,1,0:T(4,128)(2,1)S(1)}, u32[]{:S(2)}, u32[]{:S(2)}) %all-to-all-start) | async-done | bytes 294944 | tf_op jit(solution)/shard_map/all_to_all | solution.py:243
  49.0 0.0 copy-done.2
  49.0 1.6 %shard_map.84 = bf16[256,768]{1,0:T(8,128)(2,1)S(1)} custom-call(s32[1]{0:T(128)S(6)} %copy.12.count_ref, s32[1,4]{1,0:T(1,128)S(1)} %copy-done.1, s32[6]{0:T(128)S(1)} %copy-done.2, bf16[576,576]{1,0:T(8,128)(2,1)S(1)} %get-tuple-element.8.kron_ref, bf16[64,4,576]{2,1,0:T(4,128)(2,1)S(1)} %all-to-all-done.p_ref), custom_call_target="tpu_custom_call" | custom-call | tf_op jit(solution)/shard_map/pallas_call | solution.py:235
  50.6 19.9 %all_to_all.15 = bf16[16,16,768]{2,1,0:T(8,128)(2,1)S(1)} all-to-all(bf16[16,16,768]{2,1,0:T(8,128)(2,1)S(1)} %bitcast.12), channel_id=1, replica_groups=mesh['mom'=16,'en'=64] {'mom'}, dimensions={0} | all-to-all | bytes 786432 | tf_op jit(solution)/shard_map/all_to_all | solution.py:243
  70.5 1.1 %shard_map.85 = bf16[256,144]{1,0:T(8,128)(2,1)S(1)} custom-call(bf16[8,256,256]{2,1,0:T(8,128)(2,1)S(1)} %get-tuple-element.7.weight_ref, bf16[256,768]{1,0:T(8,128)(2,1)S(1)} %bitcast.13), custom_call_target="tpu_custom_call" | custom-call | tf_op jit(solution)/shard_map/pallas_call | solution.py:239
  71.6 12.4 %all_to_all.16 = bf16[16,16,144]{2,1,0:T(8,128)(2,1)S(1)} all-to-all(bf16[16,16,144]{2,1,0:T(8,128)(2,1)S(1)} %bitcast.14), channel_id=1, replica_groups=mesh['mom'=16,'en'=64] {'mom'}, dimensions={0} | all-to-all | bytes 147456 | tf_op jit(solution)/shard_map/all_to_all | solution.py:243
  84.0 0.8 reshape.27
  (1 shorter events, 0.0 us)
Async XLA Ops:
  0.0 33.1 %copy-start.3 = (f32[1,4,12,12]{3,1,2,0:T(4,128)S(1)}, f32[1,4,12,12]{3,1,2,0:T(4,128)}, u32[]{:S(2)}) copy-start(f32[1,4,12,12]{3,1,2,0:T(4,128)} %param.15) | copy-start | bytes 6916
  0.0 33.1 %copy-start.1 = (s32[1,4]{1,0:T(1,128)S(1)}, s32[1,4]{1,0:T(1,128)}, u32[]{:S(2)}) copy-start(s32[1,4]{1,0:T(1,128)} %mode_ref.3) | copy-start | bytes 52
  0.0 33.1 %copy-start = (f32[16,6]{0,1:T(8,128)S(1)}, f32[16,6]{0,1:T(8,128)}, u32[]{:S(2)}) copy-start(f32[16,6]{0,1:T(8,128)} %param.14) | copy-start | bytes 1156
  0.0 49.0 %copy-start.2 = (s32[6]{0:T(128)S(1)}, s32[6]{0:T(128)}, u32[]{:S(2)}) copy-start(s32[6]{0:T(128)} %shift_ref.1) | copy-start | bytes 76
  8.0 41.1 %all-to-all-start = ((bf16[64,4,576]{2,1,0:T(4,128)(2,1)}), bf16[64,4,576]{2,1,0:T(4,128)(2,1)S(1)}, u32[]{:S(2)}, u32[]{:S(2)}) async-start(bf16[64,4,576]{2,1,0:T(4,128)(2,1)} %shard_map.83), calls=%async_computation | async-start | bytes 655360 | tf_op jit(solution)/shard_map/all_to_all | solution.py:243

commit v3 on v2

v3 whole, which is shorter than its diff:
```python
import functools

import jax
import jax.numpy as jnp
from jax import lax
from jax.experimental import pallas as pl
from jax.experimental.pallas import tpu as pltpu
from jax.sharding import PartitionSpec as P

F32, BF16, I32 = jnp.float32, jnp.bfloat16, jnp.int32
NO, NX, ATOMS, ROWS, ORD = 12, 144, 64, 256, 768
HALF, SUB, WIN = 384, 192, 256


def iota(shape, dim):
    return lax.broadcasted_iota(I32, shape, dim)


def one(mask):
    return jnp.where(mask, 1.0, 0.0).astype(BF16)


def dot(a, b):
    return lax.dot_general(a, b, (((1,), (0,)), ((), ())), preferred_element_type=F32)


def dot_t(a, b):
    return lax.dot_general(a, b, (((1,), (1,)), ((), ())), preferred_element_type=F32)


def pick_lanes(parts):
    lane = iota((ROWS, 128), 1)
    tiles = [parts[0][:, :128]]
    for t in range(1, 4):
        tiles.append(jnp.where(lane < 16 * t, parts[t - 1][:, 128:], parts[t][:, :128]))
    tiles.append(parts[3][:, 128:])
    return tiles


def atom_of(index):
    return (index * 5462) >> 16


def orbital_of(index):
    return index - NO * atom_of(index)


def blocks_kernel(nb_hbm, s_hbm, g_hbm, out_ref, nb_ref, s_ref, g_ref, left_ref, z_ref, sems):
    small = [pltpu.make_async_copy(s_hbm, s_ref, sems.at[4]), pltpu.make_async_copy(nb_hbm, nb_ref, sems.at[5])]
    copies = []
    for t in range(2):
        for part in range(2):
            rows = pl.ds(HALF * t, HALF)
            copies.append(
                pltpu.make_async_copy(g_hbm.at[part, rows, :], g_ref.at[part, rows, :], sems.at[2 * t + part])
            )
    for copy in small + copies:
        copy.start()
    for copy in small:
        copy.wait()
    s_r = s_ref[:, 0, :].astype(F32)
    s_i = s_ref[:, 1, :].astype(F32)
    tall, thin = iota((128, 128), 0), iota((128, NO), 0)
    wide, slot = iota((1, 128), 1), iota((1, NO), 1)
    factors = []
    for t in range(6):
        cols = slice(128 * t, 128 * (t + 1))
        upper = jnp.concatenate([s_r[:, cols], s_i[:, cols]], axis=1).astype(BF16)
        lower = jnp.concatenate([-s_i[:, cols], s_r[:, cols]], axis=1).astype(BF16)
        mine = atom_of(wide + (128 * t + 240))
        for kind in range(2):
            if kind:
                near = tall + jnp.where(tall < 64, 128 * (t + 1) + 240, 128 * (t - 1) + 240)
                pick = thin + jnp.where(thin < 64, 128 * (t + 1) + 240, 128 * (t - 1) + 240)
            else:
                near, pick = tall + (128 * t + 240), thin + (128 * t + 240)
            spread = one(orbital_of(pick) == slot)
            same = atom_of(near) == mine
            same = jnp.concatenate([same, same], axis=1)
            halves = [jnp.where(same, dot(spread, x), 0.0).astype(BF16) for x in (upper, lower)]
            factors.append(jnp.concatenate(halves, axis=0))
    lane = iota((HALF, 128), 1)
    for half in range(2):
        rows = slice(HALF * half, HALF * (half + 1))
        copies[2 * half].wait()
        copies[2 * half + 1].wait()
        tiles = [[g_ref[part, rows, 128 * t : 128 * (t + 1)] for part in range(2)] for t in range(6)]
        for t in range(6):
            low, high = tiles[max(t - 1, 0)], tiles[min(t + 1, 5)]
            beside = [jnp.where(lane < 64, high[part], low[part]) for part in range(2)]
            line = dot(jnp.concatenate(tiles[t], axis=1), factors[2 * t])
            line += dot(jnp.concatenate(beside, axis=1), factors[2 * t + 1])
            line = line.astype(BF16)
            left_ref[0, rows, 256 * t : 256 * t + 256] = line
            left_ref[1, rows, 256 * t : 256 * t + 128] = line[:, 128:]
            left_ref[1, rows, 256 * t + 128 : 256 * t + 256] = -line[:, :128]
    own = atom_of(iota((1, NX), 1)) == orbital_of(iota((SUB, NX), 0))

    def products(half, odd):
        mine = slice(HALF * half + SUB * odd, HALF * half + SUB * (odd + 1))
        window = slice(HALF * half + 128 * odd, HALF * half + 128 * odd + WIN)
        stacked = jnp.concatenate([left_ref[0, mine, :], left_ref[1, mine, :]], axis=0)
        cols = [slice(128 * t, 128 * (t + 1)) for t in range(6)]
        right = jnp.concatenate([g_ref[part, window, col] for col in cols for part in range(2)], axis=1)
        return dot_t(stacked, right)

    def finish(half, odd, lesser):
        base = HALF * half
        square = slice(base + 128 * odd, base + 128 * odd + WIN)
        inner = slice(64 * odd, 64 * odd + SUB)
        shift = []
        for part, sign in ((0, -1.0), (1, 1.0)):
            plain = g_ref[part, square, square].astype(F32)
            shift.append(plain[inner] + sign * plain.T[inner])
        row, col = iota((SUB, WIN), 0) + SUB * odd, iota((1, WIN), 1) + 128 * odd
        diagonal = atom_of(row) == atom_of(col)
        fold = one(orbital_of(iota((WIN, NX), 0) + 128 * odd) == orbital_of(iota((1, NX), 1)))
        values = [lesser[:SUB], lesser[SUB:], jnp.where(row > col, shift[0], shift[1])]
        for c, value in enumerate(values):
            folded = dot(jnp.where(diagonal, value, 0.0).astype(BF16), fold)
            z_ref[c, base + SUB * odd : base + SUB * (odd + 1), :] = jnp.where(own, folded, 0.0).astype(BF16)

    todo = [(0, 0), (0, 1), (1, 0), (1, 1)]
    ahead = products(*todo[0])
    for w in range(4):
        lesser = ahead
        if w < 3:
            ahead = products(*todo[w + 1])
        finish(*todo[w], lesser)
    gather = one(atom_of(iota((ATOMS, ORD), 1)) == iota((ATOMS, ORD), 0))
    blocks = jnp.concatenate([dot(gather, z_ref[c]) for c in range(3)], axis=1).astype(BF16)
    owner = one(iota((ROWS, ATOMS), 0) >> 2 == iota((ROWS, ATOMS), 1))
    atoms = dot_t(owner, nb_ref[...].astype(F32).astype(BF16)).astype(I32)
    bond = iota((ROWS, 1), 0) & 3
    wanted = atoms[:, 0:1]
    for m in range(1, 4):
        wanted = jnp.where(bond == m, atoms[:, m : m + 1], wanted)
    sent = dot(one(iota((ROWS, ATOMS), 1) == wanted), blocks)
    out_ref[...] = sent.reshape(ATOMS, 4, 3 * NX).astype(BF16)


def prepare_kernel(count_ref, mode_ref, shift_ref, n_ref, c_ref, kron_ref, weight_ref, turn_ref, move_ref, step_ref, fold_ref):
    factors = []
    for outer in (True, False):
        pieces = []
        for m in range(4):
            x = iota((NO, WIN), 1) - 16 * m
            inside = (x >= 0) & (x < NX)
            wide = (atom_of if outer else orbital_of)(jnp.maximum(x, 0))
            spread = jnp.where(inside & (iota((NO, WIN), 0) == wide), 1.0, 0.0)
            pieces.append(
                lax.dot_general(
                    c_ref[m].T, spread, (((1,), (0,)), ((), ())), precision=lax.Precision.HIGHEST, preferred_element_type=F32
                )
            )
        wide = jnp.concatenate(pieces, axis=0)
        high = wide.astype(BF16)
        rest = wide - high.astype(F32)
        middle = rest.astype(BF16)
        low = (rest - middle.astype(F32)).astype(BF16)
        stacked = jnp.concatenate([high, middle, low], axis=0)
        row = iota((4 * NX, 3 * 48), 0)
        j = atom_of(row)
        source = j if outer else NO * (atom_of(j)) + row - NO * j
        factors.append(dot(one(orbital_of(iota((1, 3 * 48), 1)) + NO * (atom_of(iota((1, 3 * 48), 1)) & 3) == source), stacked))
    kron_ref[...] = (factors[0] * factors[1]).astype(BF16)
    row, lane = iota((16, ROWS), 0), iota((16, ROWS), 1)
    transfer = (row - lane // 16) & 15
    spread = one(iota((ROWS, 16), 0) // 16 == iota((ROWS, 16), 1))
    same = (iota((ROWS, ROWS), 0) & 15) == (iota((ROWS, ROWS), 1) & 15)
    for m in range(4):
        weights = jnp.zeros((16, ROWS), F32)
        for q in range(16):
            weights = jnp.where(transfer == q, n_ref[mode_ref[0, m], q] * (1.0 / 16), weights)
        high = weights.astype(BF16)
        low = (weights - high.astype(F32)).astype(BF16)
        for i, part in enumerate((high, low)):
            weight_ref[2 * m + i] = jnp.where(same, dot(spread, part), 0.0).astype(BF16)
    row, column = iota((ROWS, ROWS), 0), iota((ROWS, ROWS), 1)
    turn_ref[...] = one(column == ((row & 63) << 2) + (row >> 6))
    x = iota((1, NX), 1)
    upper = orbital_of(x)
    swapped = NO * upper + atom_of(x)
    below = upper < atom_of(x)
    lane = iota((WIN, NX), 0)
    for c in range(2):
        move_ref[c] = one(lane == x + 16 * c)
    kept = jnp.where(lane - 32 == x, 1.0, 0.0)
    turned = jnp.where(lane - 32 == swapped, 1.0, 0.0)
    move_ref[2] = jnp.where(below, kept, jnp.where(x == swapped, 0.0, -turned)).astype(BF16)
    move_ref[3] = jnp.where(below, turned, kept).astype(BF16)
    part = (row & 3) - (column >> 6)
    gap = (column & 63) - (row >> 2)
    gap = jnp.where((part == 0) | (part == 2), gap, 8 * ROWS)
    facing = jnp.where((row & 2) > 0, -gap, gap)
    gap = jnp.abs(gap)
    for m in range(4):
        step = jnp.where(m < count_ref[0], shift_ref[mode_ref[0, m]], 4 * ROWS)
        step_ref[m, :ROWS, :] = one(gap == step)
        step_ref[m, ROWS:, :] = one(facing == step)
    lane, target = iota((640, WIN), 0), iota((1, WIN), 1) - 64
    source = lane
    for m in range(3):
        source = jnp.where(source >= NX, source - NX, source)
    fold_ref[...] = one((source == target) & (target < NX))


def image_kernel(kron_ref, turn_ref, move_ref, step_ref, fold_ref, p_ref, out_ref):
    pieces = p_ref[...].astype(F32).reshape(ROWS, 3 * NX).astype(BF16)
    pieces = dot(turn_ref[...], pieces).astype(BF16)
    parts = [dot(pieces[:, 128 * c : 128 * c + WIN], move_ref[c]).astype(BF16) for c in range(2)]
    parts += [dot(pieces[:, WIN:], move_ref[c, :176, :]).astype(BF16) for c in (2, 3)]
    windows = []
    for m in range(4):
        bond = jnp.concatenate([value[ATOMS * m : ATOMS * (m + 1)] for value in parts], axis=0)
        windows.append(dot(bond, kron_ref[NX * m : NX * (m + 1), :]).astype(BF16))
    shifted = [dot(step_ref[m], windows[m]) for m in range(4)]
    tiles = pick_lanes([both[:ROWS] for both in shifted])
    sums = jnp.concatenate(pick_lanes([both[ROWS:] for both in shifted]), axis=1).astype(BF16)
    total = dot(sums, fold_ref[...])
    last = jnp.where(iota((ROWS, 128), 1) < 64, tiles[4], total[:, :128])
    for t, tile in enumerate([*tiles[:4], last, total[:, 128:]]):
        out_ref[:, 128 * t : 128 * (t + 1)] = tile.astype(BF16)


def momentum_kernel(weight_ref, v_ref, out_ref):
    same = (iota((ROWS, ROWS), 0) & 15) == (iota((ROWS, ROWS), 1) & 15)
    acc = jnp.zeros((ROWS, NX), F32)
    for m in range(5):
        window = v_ref[:, 128 * m : 128 * m + WIN]
        move = one(iota((WIN, NX), 0) == iota((WIN, NX), 1) + 16 * m)
        pieces = dot(window, move).astype(BF16)
        if m == 4:
            acc += dot(jnp.where(same, 1.0 / 16, 0.0).astype(BF16), pieces)
        else:
            acc += dot(weight_ref[2 * m], pieces) + dot(weight_ref[2 * m + 1], pieces)
    out_ref[...] = acc.astype(BF16)


VMEM = pl.BlockSpec(memory_space=pltpu.VMEM)
SMEM = pl.BlockSpec(memory_space=pltpu.SMEM)
HBM = pl.BlockSpec(memory_space=pltpu.HBM)


def call(kernel, outs, specs, scratch=()):
    shapes = [jax.ShapeDtypeStruct(out, BF16) for out in outs]
    return pl.pallas_call(
        kernel,
        out_shape=shapes if len(outs) > 1 else shapes[0],
        in_specs=specs,
        out_specs=[VMEM] * len(outs) if len(outs) > 1 else VMEM,
        scratch_shapes=scratch,
        compiler_params=pltpu.CompilerParams(vmem_limit_bytes=48 << 20),
    )


def blocks_of(neighbours, retarded, injection):
    scratch = [
        pltpu.VMEM((4, ATOMS), I32),
        pltpu.VMEM((NO, 2, ORD), BF16),
        pltpu.VMEM((2, ORD, ORD), BF16),
        pltpu.VMEM((2, ORD, 2 * ORD), BF16),
        pltpu.VMEM((3, ORD, NX), BF16),
        pltpu.SemaphoreType.DMA((6,)),
    ]
    f = call(blocks_kernel, [(ATOMS, 4, 3 * NX)], [HBM, HBM, HBM], scratch)
    operands = (neighbours.T, jnp.swapaxes(injection, 0, 1), retarded)
    return f(*(pltpu.with_memory_space_constraint(x, pltpu.HBM) for x in operands))


def prepared(bond_count, bond_mode, mode_shift, occupation, coupling):
    outs = [(4 * NX, WIN), (8, ROWS, ROWS), (ROWS, ROWS), (4, WIN, NX), (4, 2 * ROWS, ROWS), (640, WIN)]
    f = call(prepare_kernel, outs, [SMEM, SMEM, SMEM, SMEM, VMEM])
    return f(bond_count, bond_mode, mode_shift, occupation.T, coupling)


def image_of(kron, turn, move, step, fold, pieces):
    return call(image_kernel, [(ROWS, ORD)], [VMEM] * 6)(kron, turn, move, step, fold, pieces)


def convolved(weights, pieces):
    return call(momentum_kernel, [(ROWS, NX)], [VMEM, VMEM])(weights, pieces)


def exchange(x, axis):
    return lax.all_to_all(x, axis, split_axis=0, concat_axis=0, tiled=True)


def per_device(retarded, injection, neighbours, bond_count, bond_mode, mode_shift, occupation, coupling):
    sent = blocks_of(neighbours, retarded[0, 0], injection[0, 0])
    kron, weights, *selectors = prepared(bond_count, bond_mode, mode_shift, occupation, coupling[0])
    pieces = exchange(sent, "en")
    imaged = image_of(kron, *selectors, pieces)
    spread = exchange(imaged.reshape(16, 16, ORD), "mom")
    scattered = convolved(weights, spread.reshape(ROWS, ORD))
    back = exchange(scattered.reshape(16, 16, NX), "mom")
    return back.reshape(1, 1, ATOMS, 4, NX).astype(F32)


def solution(mesh):
    en = P("en")
    in_specs = (
        P("mom", "en", None, None, None),
        P("mom", "en", None, None, None),
        P(),
        en,
        P("en", None),
        P(),
        P(),
        P("en", None, None, None),
    )
    return jax.shard_map(
        per_device,
        mesh=mesh,
        in_specs=in_specs,
        out_specs=P("mom", "en", None, None, None),
        check_vma=False,
    )
```

time: 85.1 us -> 82.8 us (0.973)
  Pallas kernels: 12.9 us -> 10.6 us
  local copies, waits for them, and re-layouts: 0.8 us -> 2.35 us
  waiting for transfers between devices: 13.6 us -> 12.1 us
    pallas_call x1, Pallas kernels: 7.93 us -> 6.23 us  [blocks_of(): f(*(pltpu.with_memory_space_constraint(x, pltpu.HBM) for x in operands))]
    all_to_all x1, waiting for transfers between devices: 13.6 us -> 12.1 us  [exchange(): return lax.all_to_all(x, axis, split_axis=0, concat_axis=0, tiled=True)]
    unnamed x9 -> x13, local copies, waits for them, and re-layouts: 0.02 us -> 1.57 us
  transfers between devices with their start and end apart: 1 -> 1, of which waited for: 1 -> 1; matrix products, arithmetic and copies ran while one was open for 0% -> 0% of each run, Pallas kernels for 3% -> 2%
where the time goes in v3:
time: 82.8 us; the launch traced here: 82.5 us
  blocking collectives  32.3 us (39%)
  starting transfers between devices  24.5 us (30%)
  waiting for transfers between devices  12.1 us (15%)
  Pallas kernels  10.6 us (13%)
  local copies, waits for them, and re-layouts  2.35 us (3%)
    all_to_all x2, blocking collectives, exchange(): return lax.all_to_all(x, axis, split_axis=0, concat_axis=0, tiled=True)  32.3 us
    all_to_all x1, starting transfers between devices, exchange(): return lax.all_to_all(x, axis, split_axis=0, concat_axis=0, tiled=True)  24.5 us
    all_to_all x1, waiting for transfers between devices, exchange(): return lax.all_to_all(x, axis, split_axis=0, concat_axis=0, tiled=True)  12.1 us
    pallas_call x1, Pallas kernels, blocks_of(): f(*(pltpu.with_memory_space_constraint(x, pltpu.HBM) for x in operands))  6.23 us
    pallas_call x1, Pallas kernels, prepared(): return f(bond_count, bond_mode, mode_shift, occupation.T, coupling)  1.99 us
  transfers between devices with their start and end apart: 1, of which 1 were waited for; matrix products, arithmetic and copies ran while one was open for 0% of the time, Pallas kernels for 2%

profile of v3, /device:TPU:1, one launch (start us, length us, event | category | flops | bytes accessed | tf_op | source)
XLA Modules:
  0.0 82.5 jit_solution(2838983841806468331)
XLA Ops:
  0.0 0.0 copy-start.5
  0.0 0.0 copy-start.2
  0.0 0.0 copy-start.4
  0.0 0.0 copy-start.3
  0.0 6.2 %shard_map.83 = bf16[64,4,432]{2,1,0:T(4,128)(2,1)} custom-call(s32[4,64]{1,0:T(4,128)} %bitcast.19, bf16[12,2,768]{2,1,0:T(2,128)(2,1)} %bitcast.18, bf16[2,768,768]{2,1,0:T(8,128)(2,1)} %bitcast.17), custom_call_target="tpu_custom_call" | custom-call | tf_op jit(solution)/shard_map/pallas_call | solution.py:268
  6.3 24.5 %all-to-all-start = ((bf16[64,4,432]{2,1,0:T(4,128)(2,1)}), bf16[64,4,432]{2,1,0:T(4,128)(2,1)S(1)}, u32[]{:S(2)}, u32[]{:S(2)}) async-start(bf16[64,4,432]{2,1,0:T(4,128)(2,1)} %shard_map.83), calls=%async_computation | async-start | bytes 524288 | tf_op jit(solution)/shard_map/all_to_all | solution.py:286
  31.4 0.0 copy-done.5
  31.4 0.0 copy-done.2
  31.4 0.0 copy-done.4
  31.4 0.0 copy-done.3
  31.4 2.0 %shard_map.82 = (bf16[576,256]{1,0:T(8,128)(2,1)S(1)}, bf16[8,256,256]{2,1,0:T(8,128)(2,1)S(1)}, bf16[256,256]{1,0:T(8,128)(2,1)S(1)}, bf16[4,256,144]{2,1,0:T(8...) custom-call(s32[1]{0:T(128)S(6)} %copy.12.count_ref, s32[1,4]{1,0:T(1,128)S(1)} %copy-done.3, ...), custom_call_target="tpu_custom_call" | custom-call | tf_op jit(solution)/shard_map/pallas_call | solution.py:274
  33.4 0.0 copy-start
  33.4 0.6 copy-done
  34.1 12.1 %all-to-all-done.p_ref = bf16[64,4,432]{2,1,0:T(4,128)(2,1)S(1)} async-done(((bf16[64,4,432]{2,1,0:T(4,128)(2,1)}), bf16[64,4,432]{2,1,0:T(4,128)(2,1)S(1)}, u32[]{:S(2)}, u32[]{:S(2)}) %all-to-all-start) | async-done | bytes 221216 | tf_op jit(solution)/shard_map/all_to_all | solution.py:286
  46.1 0.0 copy-start.1
  46.2 0.9 %copy-done.1 = bf16[256,256]{1,0:T(8,128)(2,1)S(1)} copy-done((bf16[256,256]{1,0:T(8,128)(2,1)S(1)}, bf16[256,256]{1,0:T(8,128)(2,1)}, u32[]{:S(2)}) %copy-start.1) | copy-done | bytes 131096
  47.1 1.2 %shard_map.84 = bf16[256,768]{1,0:T(8,128)(2,1)S(1)} custom-call(bf16[576,256]{1,0:T(8,128)(2,1)S(1)} %get-tuple-element.12.kron_ref, bf16[256,256]{1,0:T(8,128)(2,1)S(1)} %copy-done.1, bf16[4,256,144]{2,1,0:T(8,128)(2,1)S(1)} %get-tuple-element.14.move_ref, bf16[4,512,256]{2,1,0:T(8,128)(2,1)S(1)} %get-tuple-element.15.step_ref, ...), custom_call_target="tpu_custom_call" | custom-call | tf_op jit(solution)/shard_map/pallas_call | solution.py:278
  48.3 19.9 %all_to_all.15 = bf16[16,16,768]{2,1,0:T(8,128)(2,1)S(1)} all-to-all(bf16[16,16,768]{2,1,0:T(8,128)(2,1)S(1)} %bitcast.13), channel_id=1, replica_groups=mesh['mom'=16,'en'=64] {'mom'}, dimensions={0} | all-to-all | bytes 786432 | tf_op jit(solution)/shard_map/all_to_all | solution.py:286
  68.1 1.1 %shard_map.85 = bf16[256,144]{1,0:T(8,128)(2,1)S(1)} custom-call(bf16[8,256,256]{2,1,0:T(8,128)(2,1)S(1)} %get-tuple-element.11.weight_ref, bf16[256,768]{1,0:T(8,128)(2,1)S(1)} %bitcast.12), custom_call_target="tpu_custom_call" | custom-call | tf_op jit(solution)/shard_map/pallas_call | solution.py:282
  69.3 12.4 %all_to_all.16 = bf16[16,16,144]{2,1,0:T(8,128)(2,1)S(1)} all-to-all(bf16[16,16,144]{2,1,0:T(8,128)(2,1)S(1)} %bitcast.14), channel_id=1, replica_groups=mesh['mom'=16,'en'=64] {'mom'}, dimensions={0} | all-to-all | bytes 147456 | tf_op jit(solution)/shard_map/all_to_all | solution.py:286
  81.7 0.8 reshape.27
  (1 shorter events, 0.0 us)
Async XLA Ops:
  0.0 31.4 %copy-start.5 = (f32[1,4,12,12]{3,1,2,0:T(4,128)S(1)}, f32[1,4,12,12]{3,1,2,0:T(4,128)}, u32[]{:S(2)}) copy-start(f32[1,4,12,12]{3,1,2,0:T(4,128)} %param.15) | copy-start | bytes 6916
  0.0 31.4 %copy-start.2 = (f32[16,6]{0,1:T(8,128)S(1)}, f32[16,6]{0,1:T(8,128)}, u32[]{:S(2)}) copy-start(f32[16,6]{0,1:T(8,128)} %param.14) | copy-start | bytes 1156
  0.0 31.4 %copy-start.4 = (s32[6]{0:T(128)S(1)}, s32[6]{0:T(128)}, u32[]{:S(2)}) copy-start(s32[6]{0:T(128)} %shift_ref.1) | copy-start | bytes 76
  0.0 31.4 %copy-start.3 = (s32[1,4]{1,0:T(1,128)S(1)}, s32[1,4]{1,0:T(1,128)}, u32[]{:S(2)}) copy-start(s32[1,4]{1,0:T(1,128)} %mode_ref.1) | copy-start | bytes 52
  6.3 39.9 %all-to-all-start = ((bf16[64,4,432]{2,1,0:T(4,128)(2,1)}), bf16[64,4,432]{2,1,0:T(4,128)(2,1)S(1)}, u32[]{:S(2)}, u32[]{:S(2)}) async-start(bf16[64,4,432]{2,1,0:T(4,128)(2,1)} %shard_map.83), calls=%async_computation | async-start | bytes 524288 | tf_op jit(solution)/shard_map/all_to_all | solution.py:286
  33.4 0.7 copy-start
  46.1 0.9 %copy-start.1 = (bf16[256,256]{1,0:T(8,128)(2,1)S(1)}, bf16[256,256]{1,0:T(8,128)(2,1)}, u32[]{:S(2)}) copy-start(bf16[256,256]{1,0:T(8,128)(2,1)} %copy-done) | copy-start | bytes 393220

commit v4 on v3

--- a/solution.py
+++ b/solution.py
@@ -26,15 +26,6 @@
 
 def dot_t(a, b):
     return lax.dot_general(a, b, (((1,), (1,)), ((), ())), preferred_element_type=F32)
-
-
-def pick_lanes(parts):
-    lane = iota((ROWS, 128), 1)
-    tiles = [parts[0][:, :128]]
-    for t in range(1, 4):
-        tiles.append(jnp.where(lane < 16 * t, parts[t - 1][:, 128:], parts[t][:, :128]))
-    tiles.append(parts[3][:, 128:])
-    return tiles
 
 
 def atom_of(index):
@@ -139,102 +130,155 @@
     out_ref[...] = sent.reshape(ATOMS, 4, 3 * NX).astype(BF16)
 
 
-def prepare_kernel(count_ref, mode_ref, shift_ref, n_ref, c_ref, kron_ref, weight_ref, turn_ref, move_ref, step_ref, fold_ref):
+def prepare_kernel(
+    count_ref,
+    mode_ref,
+    shift_ref,
+    n_ref,
+    c_ref,
+    kron_ref,
+    turn_ref,
+    part_ref,
+    pair_ref,
+    single_ref,
+    weight_ref,
+    move_ref,
+    unpack_ref,
+):
+    lane = iota((1, WIN), 1)
+    entry = jnp.where(lane < 128, lane, 128 + (lane & 15))
     factors = []
     for outer in (True, False):
-        pieces = []
-        for m in range(4):
-            x = iota((NO, WIN), 1) - 16 * m
-            inside = (x >= 0) & (x < NX)
-            wide = (atom_of if outer else orbital_of)(jnp.maximum(x, 0))
-            spread = jnp.where(inside & (iota((NO, WIN), 0) == wide), 1.0, 0.0)
-            pieces.append(
-                lax.dot_general(
-                    c_ref[m].T, spread, (((1,), (0,)), ((), ())), precision=lax.Precision.HIGHEST, preferred_element_type=F32
-                )
-            )
-        wide = jnp.concatenate(pieces, axis=0)
-        high = wide.astype(BF16)
-        rest = wide - high.astype(F32)
+        wide = (atom_of if outer else orbital_of)(entry)
+        spread = jnp.where(iota((NO, WIN), 0) == wide, 1.0, 0.0)
+        stacked = lax.dot_general(
+            jnp.concatenate([c_ref[m].T for m in range(4)], axis=0),
+            spread,
+            (((1,), (0,)), ((), ())),
+            precision=lax.Precision.HIGHEST,
+            preferred_element_type=F32,
+        )
+        high = stacked.astype(BF16)
+        rest = stacked - high.astype(F32)
         middle = rest.astype(BF16)
         low = (rest - middle.astype(F32)).astype(BF16)
-        stacked = jnp.concatenate([high, middle, low], axis=0)
         row = iota((4 * NX, 3 * 48), 0)
         j = atom_of(row)
-        source = j if outer else NO * (atom_of(j)) + row - NO * j
-        factors.append(dot(one(orbital_of(iota((1, 3 * 48), 1)) + NO * (atom_of(iota((1, 3 * 48), 1)) & 3) == source), stacked))
+        source = j if outer else NO * atom_of(j) + row - NO * j
+        column = iota((1, 3 * 48), 1)
+        column = orbital_of(column) + NO * (atom_of(column) & 3)
+        factors.append(dot(one(column == source), jnp.concatenate([high, middle, low], axis=0)))
     kron_ref[...] = (factors[0] * factors[1]).astype(BF16)
-    row, lane = iota((16, ROWS), 0), iota((16, ROWS), 1)
-    transfer = (row - lane // 16) & 15
-    spread = one(iota((ROWS, 16), 0) // 16 == iota((ROWS, 16), 1))
-    same = (iota((ROWS, ROWS), 0) & 15) == (iota((ROWS, ROWS), 1) & 15)
-    for m in range(4):
-        weights = jnp.zeros((16, ROWS), F32)
-        for q in range(16):
-            weights = jnp.where(transfer == q, n_ref[mode_ref[0, m], q] * (1.0 / 16), weights)
-        high = weights.astype(BF16)
-        low = (weights - high.astype(F32)).astype(BF16)
-        for i, part in enumerate((high, low)):
-            weight_ref[2 * m + i] = jnp.where(same, dot(spread, part), 0.0).astype(BF16)
     row, column = iota((ROWS, ROWS), 0), iota((ROWS, ROWS), 1)
     turn_ref[...] = one(column == ((row & 63) << 2) + (row >> 6))
-    x = iota((1, NX), 1)
-    upper = orbital_of(x)
-    swapped = NO * upper + atom_of(x)
-    below = upper < atom_of(x)
-    lane = iota((WIN, NX), 0)
+    x = iota((1, WIN), 1)
+    swapped = NO * orbital_of(x) + atom_of(x)
+    below = orbital_of(x) < atom_of(x)
+    lane = iota((WIN, WIN), 0)
     for c in range(2):
-        move_ref[c] = one(lane == x + 16 * c)
-    kept = jnp.where(lane - 32 == x, 1.0, 0.0)
-    turned = jnp.where(lane - 32 == swapped, 1.0, 0.0)
-    move_ref[2] = jnp.where(below, kept, jnp.where(x == swapped, 0.0, -turned)).astype(BF16)
-    move_ref[3] = jnp.where(below, turned, kept).astype(BF16)
-    part = (row & 3) - (column >> 6)
-    gap = (column & 63) - (row >> 2)
-    gap = jnp.where((part == 0) | (part == 2), gap, 8 * ROWS)
-    facing = jnp.where((row & 2) > 0, -gap, gap)
-    gap = jnp.abs(gap)
+        part_ref[c] = one((lane == x + 16 * c) & (x < NX))
+    kept = jnp.where((lane - 32 == x) & (x < NX), 1.0, 0.0)
+    turned = jnp.where((lane - 32 == swapped) & (x < NX), 1.0, 0.0)
+    part_ref[2] = jnp.where(below, kept, jnp.where(x == swapped, 0.0, -turned)).astype(BF16)
+    part_ref[3] = jnp.where(below, turned, kept).astype(BF16)
+    part = (row >> 6) - (column >> 6)
+    gap = (column & 63) - (row & 63)
+    alone = jnp.abs(jnp.where(part == 0, gap, 8 * ROWS))
+    facing = jnp.where((row & 128) > 0, -gap, gap)
+    facing = jnp.where((part == 0) | (part == 2), facing, 8 * ROWS)
     for m in range(4):
         step = jnp.where(m < count_ref[0], shift_ref[mode_ref[0, m]], 4 * ROWS)
-        step_ref[m, :ROWS, :] = one(gap == step)
-        step_ref[m, ROWS:, :] = one(facing == step)
-    lane, target = iota((640, WIN), 0), iota((1, WIN), 1) - 64
-    source = lane
-    for m in range(3):
-        source = jnp.where(source >= NX, source - NX, source)
-    fold_ref[...] = one((source == target) & (target < NX))
-
-
-def image_kernel(kron_ref, turn_ref, move_ref, step_ref, fold_ref, p_ref, out_ref):
+        pair_ref[m] = one(alone == step)
+        single_ref[m] = one(facing == step)
+    lane = iota((16, ROWS), 1)
+    transfer = ((iota((16, ROWS), 0) - ((lane & 63) >> 2)) & 15) + ((lane >> 6) << 4)
+    weights = jnp.zeros((16, ROWS), F32)
+    for m in range(4):
+        for q in range(16):
+            weights = jnp.where(transfer == 16 * m + q, n_ref[mode_ref[0, m], q] * (1.0 / 16), weights)
+    high = weights.astype(BF16)
+    low = (weights - high.astype(F32)).astype(BF16)
+    spread = one(iota((ATOMS, 16), 0) >> 2 == iota((ATOMS, 16), 1))
+    same = (iota((ATOMS, ROWS), 0) & 3) == (iota((ATOMS, ROWS), 1) & 3)
+    weight_ref[:ATOMS, :] = jnp.where(same, dot(spread, high), 0.0).astype(BF16)
+    weight_ref[ATOMS:, :] = jnp.where(same, dot(spread, low), 0.0).astype(BF16)
+    lane, target = iota((WIN, 640), 0), iota((1, 640), 1)
+    tile, slot = target >> 7, (target >> 4) & 7
+    wanted = jnp.where(tile < 4, 3 * tile + jnp.where(slot == 4, 2, slot & 1), 12 + slot)
+    wanted = jnp.where(slot < jnp.where(tile < 4, 5, 4), wanted, -1)
+    move_ref[...] = one((lane >> 4 == wanted) & ((lane & 15) == (target & 15)))
+    lane, target = iota((WIN, HALF), 0), iota((1, HALF), 1)
+    source = jnp.where(lane < 128, lane, jnp.where((lane >= 192) & (lane < 208), lane - 64, -1))
+    slot = (target - 288) >> 4
+    x = jnp.where(target < 256, target & 127, 128 + (target & 15))
+    real = (target < 128) | (slot == 0)
+    inside = (target < 256) | (slot == 0) | (slot == 1)
+    swapped = NO * orbital_of(x) + atom_of(x)
+    below = orbital_of(x) < atom_of(x)
+    kept = jnp.where(inside & (source == x), 1.0, 0.0)
+    turned = jnp.where(inside & (source == swapped), 1.0, 0.0)
+    if_real = jnp.where(below, kept, jnp.where(x == swapped, 0.0, -turned))
+    unpack_ref[...] = jnp.where(real, if_real, jnp.where(below, turned, kept)).astype(BF16)
+
+
+def image_kernel(kron_ref, turn_ref, part_ref, pair_ref, single_ref, p_ref, out_ref):
     pieces = p_ref[...].astype(F32).reshape(ROWS, 3 * NX).astype(BF16)
     pieces = dot(turn_ref[...], pieces).astype(BF16)
-    parts = [dot(pieces[:, 128 * c : 128 * c + WIN], move_ref[c]).astype(BF16) for c in range(2)]
-    parts += [dot(pieces[:, WIN:], move_ref[c, :176, :]).astype(BF16) for c in (2, 3)]
+    parts = [dot(pieces[:, 128 * c : 128 * c + WIN], part_ref[c]).astype(BF16) for c in range(2)]
+    parts += [dot(pieces[:, WIN:], part_ref[c, :176, :]).astype(BF16) for c in (2, 3)]
     windows = []
     for m in range(4):
-        bond = jnp.concatenate([value[ATOMS * m : ATOMS * (m + 1)] for value in parts], axis=0)
+        bond = jnp.concatenate([value[ATOMS * m : ATOMS * (m + 1), :NX] for value in parts], axis=0)
         windows.append(dot(bond, kron_ref[NX * m : NX * (m + 1), :]).astype(BF16))
-    shifted = [dot(step_ref[m], windows[m]) for m in range(4)]
-    tiles = pick_lanes([both[:ROWS] for both in shifted])
-    sums = jnp.concatenate(pick_lanes([both[ROWS:] for both in shifted]), axis=1).astype(BF16)
-    total = dot(sums, fold_ref[...])
-    last = jnp.where(iota((ROWS, 128), 1) < 64, tiles[4], total[:, :128])
-    for t, tile in enumerate([*tiles[:4], last, total[:, 128:]]):
-        out_ref[:, 128 * t : 128 * (t + 1)] = tile.astype(BF16)
-
-
-def momentum_kernel(weight_ref, v_ref, out_ref):
-    same = (iota((ROWS, ROWS), 0) & 15) == (iota((ROWS, ROWS), 1) & 15)
-    acc = jnp.zeros((ROWS, NX), F32)
-    for m in range(5):
-        window = v_ref[:, 128 * m : 128 * m + WIN]
-        move = one(iota((WIN, NX), 0) == iota((WIN, NX), 1) + 16 * m)
-        pieces = dot(window, move).astype(BF16)
-        if m == 4:
-            acc += dot(jnp.where(same, 1.0 / 16, 0.0).astype(BF16), pieces)
+    pairs = [dot(pair_ref[m], windows[m]) for m in range(4)]
+    totals = [dot(single_ref[m], windows[m]) for m in range(4)]
+    total = (totals[0] + totals[1]) + (totals[2] + totals[3])
+    lane = iota((1, WIN), 1)
+    entry = jnp.where(lane < 128, lane, 128 + (lane & 15))
+    below = orbital_of(entry) < atom_of(entry)
+    slot = iota((ATOMS, 128), 1) >> 4
+    rest = [jnp.zeros((ATOMS, 128), F32)] * 2
+    tiles = []
+    for p in range(16):
+        m, c = divmod(p, 3)
+        if p >= 12:
+            value = total[ATOMS * (p - 12) : ATOMS * (p - 11)]
+        elif c < 2:
+            value = pairs[m][ATOMS * c : ATOMS * (c + 1)]
         else:
-            acc += dot(weight_ref[2 * m], pieces) + dot(weight_ref[2 * m + 1], pieces)
-    out_ref[...] = acc.astype(BF16)
+            value = jnp.where(below, pairs[m][2 * ATOMS : 3 * ATOMS], pairs[m][3 * ATOMS :])
+        tiles.append(value[:, :128])
+        rest[p // 8] = jnp.where(slot == p % 8, value[:, 128:], rest[p // 8])
+    for t, tile in enumerate(tiles + rest):
+        out_ref[:, :, 128 * t : 128 * (t + 1)] = tile.reshape(16, 4, 128).astype(BF16)
+
+
+def momentum_kernel(weight_ref, move_ref, unpack_ref, v_ref, out_ref):
+    v = v_ref[...].astype(F32).reshape(ATOMS, 3 * ORD).astype(BF16)
+    rest = dot(v[:, 2048:], move_ref[...]).astype(BF16)
+    bonds = [jnp.concatenate([v[:, HALF * m : HALF * (m + 1)], rest[:, 128 * m : 128 * (m + 1)]], axis=1) for m in range(4)]
+    bonds = jnp.concatenate(bonds, axis=0)
+    lesser = jnp.concatenate([bonds[:, :256], bonds[:, :256], bonds[:, 384:]], axis=1)
+    greater = dot(bonds[:, 256:], unpack_ref[...]).astype(BF16)
+    greater = jnp.concatenate([jnp.zeros((ROWS, 256), BF16), greater], axis=1)
+    total = jnp.concatenate([v[:, 1536:2048], rest[:, 512:]], axis=1)
+    total = jnp.concatenate([total, jnp.zeros((ROWS - ATOMS, 640), BF16)], axis=0)
+    row, lane = iota((2 * ATOMS, ROWS), 0), iota((2 * ATOMS, ROWS), 1)
+    mean = ((row & 3) == (lane & 3)) & (lane < ATOMS) & (row < ATOMS)
+    mean = jnp.where(mean, 1.0 / 16, 0.0).astype(BF16)
+    weights = weight_ref[...]
+    both = dot(
+        jnp.concatenate([weights, weights, mean], axis=1), jnp.concatenate([lesser, greater, total], axis=0)
+    )
+    packed = (both[:ATOMS] + both[ATOMS:])[:, : 4 * NX]
+    out_ref[...] = packed.reshape(16, 4, 4 * NX).astype(BF16)
+
+
+def unpack_kernel(x_ref, out_ref):
+    x = x_ref[...].astype(F32).reshape(ATOMS, 4 * NX)
+    for c in range(4):
+        out_ref[:, c, :128] = x[:, 128 * c : 128 * (c + 1)]
+        out_ref[:, c, 128:] = x[:, 512 + 16 * c : 528 + 16 * c]
 
 
 VMEM = pl.BlockSpec(memory_space=pltpu.VMEM)
@@ -242,15 +286,15 @@
 HBM = pl.BlockSpec(memory_space=pltpu.HBM)
 
 
-def call(kernel, outs, specs, scratch=()):
-    shapes = [jax.ShapeDtypeStruct(out, BF16) for out in outs]
+def call(kernel, outs, specs, scratch=(), kind=BF16, limit=12):
+    shapes = [jax.ShapeDtypeStruct(out, kind) for out in outs]
     return pl.pallas_call(
         kernel,
         out_shape=shapes if len(outs) > 1 else shapes[0],
         in_specs=specs,
         out_specs=[VMEM] * len(outs) if len(outs) > 1 else VMEM,
         scratch_shapes=scratch,
-        compiler_params=pltpu.CompilerParams(vmem_limit_bytes=48 << 20),
+        compiler_params=pltpu.CompilerParams(vmem_limit_bytes=limit << 20),
     )
 
 
@@ -263,23 +307,26 @@
         pltpu.VMEM((3, ORD, NX), BF16),
         pltpu.SemaphoreType.DMA((6,)),
     ]
-    f = call(blocks_kernel, [(ATOMS, 4, 3 * NX)], [HBM, HBM, HBM], scratch)
+    f = call(blocks_kernel, [(ATOMS, 4, 3 * NX)], [HBM, HBM, HBM], scratch, limit=32)
     operands = (neighbours.T, jnp.swapaxes(injection, 0, 1), retarded)
     return f(*(pltpu.with_memory_space_constraint(x, pltpu.HBM) for x in operands))
 
 
 def prepared(bond_count, bond_mode, mode_shift, occupation, coupling):
-    outs = [(4 * NX, WIN), (8, ROWS, ROWS), (ROWS, ROWS), (4, WIN, NX), (4, 2 * ROWS, ROWS), (640, WIN)]
-    f = call(prepare_kernel, outs, [SMEM, SMEM, SMEM, SMEM, VMEM])
-    return f(bond_count, bond_mode, mode_shift, occupation.T, coupling)
-
-
-def image_of(kron, turn, move, step, fold, pieces):
-    return call(image_kernel, [(ROWS, ORD)], [VMEM] * 6)(kron, turn, move, step, fold, pieces)
+    square = (4, ROWS, ROWS)
+    for_image = [(4 * NX, WIN), (ROWS, ROWS), square, square, square]
+    for_sum = [(2 * ATOMS, ROWS), (WIN, 640), (WIN, HALF)]
+    f = call(prepare_kernel, for_image + for_sum, [SMEM, SMEM, SMEM, SMEM, VMEM])
+    outs = f(bond_count, bond_mode, mode_shift, occupation.T, coupling)
+    return outs[:5], outs[5:]
+
+
+def image_of(selectors, pieces):
+    return call(image_kernel, [(16, 4, 3 * ORD)], [VMEM] * 6)(*selectors, pieces)
 
 
 def convolved(weights, pieces):
-    return call(momentum_kernel, [(ROWS, NX)], [VMEM, VMEM])(weights, pieces)
+    return call(momentum_kernel, [(16, 4, 4 * NX)], [VMEM] * 4)(*weights, pieces)
 
 
 def exchange(x, axis):
@@ -288,13 +335,12 @@
 
 def per_device(retarded, injection, neighbours, bond_count, bond_mode, mode_shift, occupation, coupling):
     sent = blocks_of(neighbours, retarded[0, 0], injection[0, 0])
-    kron, weights, *selectors = prepared(bond_count, bond_mode, mode_shift, occupation, coupling[0])
+    selectors, weights = prepared(bond_count, bond_mode, mode_shift, occupation, coupling[0])
     pieces = exchange(sent, "en")
-    imaged = image_of(kron, *selectors, pieces)
-    spread = exchange(imaged.reshape(16, 16, ORD), "mom")
-    scattered = convolved(weights, spread.reshape(ROWS, ORD))
-    back = exchange(scattered.reshape(16, 16, NX), "mom")
-    return back.reshape(1, 1, ATOMS, 4, NX).astype(F32)
+    spread = exchange(image_of(selectors, pieces), "mom")
+    back = exchange(convolved(weights, spread), "mom")
+    out = call(unpack_kernel, [(ATOMS, 4, NX)], [VMEM], kind=F32)(back)
+    return out[None, None]
 
 
 def solution(mesh):

time: 82.8 us -> 78.6 us (0.949)
  blocking collectives: 32.3 us -> 29.5 us
  local copies, waits for them, and re-layouts: 2.35 us -> 0.02 us
    all_to_all x2, blocking collectives: 32.3 us -> 29.5 us  [exchange(): return lax.all_to_all(x, axis, split_axis=0, concat_axis=0, tiled=True)]
    unnamed x13 -> x9, local copies, waits for them, and re-layouts: 1.57 us -> 0.02 us
    pallas_call x3 -> x4, Pallas kernels: 4.35 us -> 4.54 us  [the longest x1 1.87 us: prepared(): outs = f(bond_count, bond_mode, mode_shift, occupation.T, coupling)]
where the time goes in v4:
time: 78.6 us; the launch traced here: 78.3 us
  blocking collectives  29.5 us (38%)
  starting transfers between devices  24.5 us (31%)
  waiting for transfers between devices  12.8 us (16%)
  Pallas kernels  10.8 us (14%)
    all_to_all x2, blocking collectives, exchange(): return lax.all_to_all(x, axis, split_axis=0, concat_axis=0, tiled=True)  29.5 us
    all_to_all x1, starting transfers between devices, exchange(): return lax.all_to_all(x, axis, split_axis=0, concat_axis=0, tiled=True)  24.5 us
    all_to_all x1, waiting for transfers between devices, exchange(): return lax.all_to_all(x, axis, split_axis=0, concat_axis=0, tiled=True)  12.8 us
    pallas_call x1, Pallas kernels, blocks_of(): f(*(pltpu.with_memory_space_constraint(x, pltpu.HBM) for x in operands))  6.23 us
    pallas_call x1, Pallas kernels, prepared(): outs = f(bond_count, bond_mode, mode_shift, occupation.T, coupling)  1.87 us
  transfers between devices with their start and end apart: 1, of which 1 were waited for; matrix products, arithmetic and copies ran while one was open for 0% of the time, Pallas kernels for 2%

profile of v4, /device:TPU:1, one launch (start us, length us, event | category | flops | bytes accessed | tf_op | source)
XLA Modules:
  0.0 78.3 jit_solution(2427240772914460200)
XLA Ops:
  0.0 0.0 copy-start.3
  0.0 0.0 copy-start
  0.0 0.0 copy-start.2
  0.0 0.0 copy-start.1
  0.0 6.2 %shard_map.83 = bf16[64,4,432]{2,1,0:T(4,128)(2,1)} custom-call(s32[4,64]{1,0:T(4,128)} %bitcast.14, bf16[12,2,768]{2,1,0:T(2,128)(2,1)} %bitcast.13, bf16[2,768,768]{2,1,0:T(8,128)(2,1)} %bitcast.12), custom_call_target="tpu_custom_call" | custom-call | tf_op jit(solution)/shard_map/pallas_call | solution.py:312
  6.3 24.5 %all-to-all-start = ((bf16[64,4,432]{2,1,0:T(4,128)(2,1)}), bf16[64,4,432]{2,1,0:T(4,128)(2,1)S(1)}, u32[]{:S(2)}, u32[]{:S(2)}) async-start(bf16[64,4,432]{2,1,0:T(4,128)(2,1)} %shard_map.83), calls=%async_computation | async-start | bytes 524288 | tf_op jit(solution)/shard_map/all_to_all | solution.py:333
  31.4 0.0 copy-done.3
  31.4 0.0 copy-done
  31.4 0.0 copy-done.2
  31.4 0.0 copy-done.1
  31.4 1.9 %shard_map.82 = (bf16[576,256]{1,0:T(8,128)(2,1)S(1)}, bf16[256,256]{1,0:T(8,128)(2,1)S(1)}, bf16[4,256,256]{2,1,0:T(8,128)(2,1)S(1)}, bf16[4,256,256]{2,1,0:T(8...) custom-call(s32[1]{0:T(128)S(6)} %copy.12.count_ref, ...), custom_call_target="tpu_custom_call" | custom-call | tf_op jit(solution)/shard_map/pallas_call | solution.py:320
  33.3 12.8 %all-to-all-done.p_ref = bf16[64,4,432]{2,1,0:T(4,128)(2,1)S(1)} async-done(((bf16[64,4,432]{2,1,0:T(4,128)(2,1)}), bf16[64,4,432]{2,1,0:T(4,128)(2,1)S(1)}, u32[]{:S(2)}, u32[]{:S(2)}) %all-to-all-start) | async-done | bytes 221216 | tf_op jit(solution)/shard_map/all_to_all | solution.py:333
  46.1 1.1 %shard_map.84 = bf16[16,4,2304]{2,1,0:T(4,128)(2,1)S(1)} custom-call(bf16[576,256]{1,0:T(8,128)(2,1)S(1)} %get-tuple-element.16.kron_ref, bf16[256,256]{1,0:T(8,128)(2,1)S(1)} %get-tuple-element.17.turn_ref, bf16[4,256,256]{2,1,0:T(8,128)(2,1)S(1)} %get-tuple-element.18.part_ref, bf16[4,256,256]{2,1,0:T(8,128)(2,1)S(1)} %get-tuple-element.19.pair_ref, ...), custom_call_target="tpu_custom_call" | custom-call | tf_op jit(solution)/shard_map/pallas_call | solution.py:325
  47.3 18.0 %all_to_all.15.v_ref = bf16[16,4,2304]{2,1,0:T(4,128)(2,1)S(1)} all-to-all(bf16[16,4,2304]{2,1,0:T(4,128)(2,1)S(1)} %shard_map.84), channel_id=1, replica_groups=mesh['mom'=16,'en'=64] {'mom'}, dimensions={0} | all-to-all | bytes 589824 | tf_op jit(solution)/shard_map/all_to_all | solution.py:333
  65.2 0.6 shard_map.85
  65.8 11.5 %all_to_all.16.x_ref = bf16[16,4,576]{2,1,0:T(4,128)(2,1)S(1)} all-to-all(bf16[16,4,576]{2,1,0:T(4,128)(2,1)S(1)} %shard_map.85), channel_id=1, replica_groups=mesh['mom'=16,'en'=64] {'mom'}, dimensions={0} | all-to-all | bytes 147456 | tf_op jit(solution)/shard_map/all_to_all | solution.py:333
  77.3 1.0 %shard_map.86 = f32[64,4,144]{2,1,0:T(4,128)} custom-call(bf16[16,4,576]{2,1,0:T(4,128)(2,1)S(1)} %all_to_all.16.x_ref), custom_call_target="tpu_custom_call" | custom-call | tf_op jit(solution)/shard_map/pallas_call | solution.py:342
  (1 shorter events, 0.0 us)
Async XLA Ops:
  0.0 31.4 %copy-start.3 = (f32[1,4,12,12]{3,1,2,0:T(4,128)S(1)}, f32[1,4,12,12]{3,1,2,0:T(4,128)}, u32[]{:S(2)}) copy-start(f32[1,4,12,12]{3,1,2,0:T(4,128)} %param.15) | copy-start | bytes 6916
  0.0 31.4 %copy-start = (f32[16,6]{0,1:T(8,128)S(1)}, f32[16,6]{0,1:T(8,128)}, u32[]{:S(2)}) copy-start(f32[16,6]{0,1:T(8,128)} %param.14) | copy-start | bytes 1156
  0.0 31.4 %copy-start.2 = (s32[6]{0:T(128)S(1)}, s32[6]{0:T(128)}, u32[]{:S(2)}) copy-start(s32[6]{0:T(128)} %shift_ref.1) | copy-start | bytes 76
  0.0 31.4 %copy-start.1 = (s32[1,4]{1,0:T(1,128)S(1)}, s32[1,4]{1,0:T(1,128)}, u32[]{:S(2)}) copy-start(s32[1,4]{1,0:T(1,128)} %mode_ref.1) | copy-start | bytes 52
  6.3 39.9 %all-to-all-start = ((bf16[64,4,432]{2,1,0:T(4,128)(2,1)}), bf16[64,4,432]{2,1,0:T(4,128)(2,1)S(1)}, u32[]{:S(2)}, u32[]{:S(2)}) async-start(bf16[64,4,432]{2,1,0:T(4,128)(2,1)} %shard_map.83), calls=%async_computation | async-start | bytes 524288 | tf_op jit(solution)/shard_map/all_to_all | solution.py:333

commit v5 on v4

--- a/solution.py
+++ b/solution.py
@@ -1,10 +1,9 @@
-import functools
-
 import jax
 import jax.numpy as jnp
 from jax import lax
 from jax.experimental import pallas as pl
 from jax.experimental.pallas import tpu as pltpu
+from jax.sharding import Mesh
 from jax.sharding import PartitionSpec as P
 
 F32, BF16, I32 = jnp.float32, jnp.bfloat16, jnp.int32
@@ -36,7 +35,19 @@
     return index - NO * atom_of(index)
 
 
-def blocks_kernel(nb_hbm, s_hbm, g_hbm, out_ref, nb_ref, s_ref, g_ref, left_ref, z_ref, sems):
+def en_index(place):
+    return (((place >> 1) & 7) << 3) + ((place >> 4) << 1) + (place & 1)
+
+
+def en_place(index):
+    return (((index >> 1) & 3) << 4) + ((index >> 3) << 1) + (index & 1)
+
+
+def mom_index(place):
+    return ((place & 7) << 1) + (place >> 3)
+
+
+def blocks_kernel(nb_hbm, s_hbm, g_hbm, out_ref, nb_ref, s_ref, g_ref, left_ref, z_ref, mask_ref, pick_ref, sems):
     small = [pltpu.make_async_copy(s_hbm, s_ref, sems.at[4]), pltpu.make_async_copy(nb_hbm, nb_ref, sems.at[5])]
     copies = []
     for t in range(2):
@@ -47,17 +58,9 @@
             )
     for copy in small + copies:
         copy.start()
-    for copy in small:
-        copy.wait()
-    s_r = s_ref[:, 0, :].astype(F32)
-    s_i = s_ref[:, 1, :].astype(F32)
     tall, thin = iota((128, 128), 0), iota((128, NO), 0)
     wide, slot = iota((1, 128), 1), iota((1, NO), 1)
-    factors = []
     for t in range(6):
-        cols = slice(128 * t, 128 * (t + 1))
-        upper = jnp.concatenate([s_r[:, cols], s_i[:, cols]], axis=1).astype(BF16)
-        lower = jnp.concatenate([-s_i[:, cols], s_r[:, cols]], axis=1).astype(BF16)
         mine = atom_of(wide + (128 * t + 240))
         for kind in range(2):
             if kind:
@@ -65,10 +68,21 @@
                 pick = thin + jnp.where(thin < 64, 128 * (t + 1) + 240, 128 * (t - 1) + 240)
             else:
                 near, pick = tall + (128 * t + 240), thin + (128 * t + 240)
-            spread = one(orbital_of(pick) == slot)
-            same = atom_of(near) == mine
-            same = jnp.concatenate([same, same], axis=1)
-            halves = [jnp.where(same, dot(spread, x), 0.0).astype(BF16) for x in (upper, lower)]
+            mask_ref[2 * t + kind] = one(atom_of(near) == mine)
+            pick_ref[2 * t + kind] = one(orbital_of(pick) == slot)
+    for copy in small:
+        copy.wait()
+    s_r = s_ref[:, 0, :].astype(F32)
+    s_i = s_ref[:, 1, :].astype(F32)
+    factors = []
+    for t in range(6):
+        cols = slice(128 * t, 128 * (t + 1))
+        upper = jnp.concatenate([s_r[:, cols], s_i[:, cols]], axis=1).astype(BF16)
+        lower = jnp.concatenate([-s_i[:, cols], s_r[:, cols]], axis=1).astype(BF16)
+        for kind in range(2):
+            mask = mask_ref[2 * t + kind]
+            mask = jnp.concatenate([mask, mask], axis=1)
+            halves = [dot(pick_ref[2 * t + kind], x).astype(BF16) * mask for x in (upper, lower)]
             factors.append(jnp.concatenate(halves, axis=0))
     lane = iota((HALF, 128), 1)
     for half in range(2):
@@ -120,7 +134,7 @@
         finish(*todo[w], lesser)
     gather = one(atom_of(iota((ATOMS, ORD), 1)) == iota((ATOMS, ORD), 0))
     blocks = jnp.concatenate([dot(gather, z_ref[c]) for c in range(3)], axis=1).astype(BF16)
-    owner = one(iota((ROWS, ATOMS), 0) >> 2 == iota((ROWS, ATOMS), 1))
+    owner = one(en_index(iota((ROWS, ATOMS), 0) >> 2) == iota((ROWS, ATOMS), 1))
     atoms = dot_t(owner, nb_ref[...].astype(F32).astype(BF16)).astype(I32)
     bond = iota((ROWS, 1), 0) & 3
     wanted = atoms[:, 0:1]
@@ -170,7 +184,7 @@
         factors.append(dot(one(column == source), jnp.concatenate([high, middle, low], axis=0)))
     kron_ref[...] = (factors[0] * factors[1]).astype(BF16)
     row, column = iota((ROWS, ROWS), 0), iota((ROWS, ROWS), 1)
-    turn_ref[...] = one(column == ((row & 63) << 2) + (row >> 6))
+    turn_ref[...] = one(column == (en_place(row & 63) << 2) + (row >> 6))
     x = iota((1, WIN), 1)
     swapped = NO * orbital_of(x) + atom_of(x)
     below = orbital_of(x) < atom_of(x)
@@ -191,7 +205,8 @@
         pair_ref[m] = one(alone == step)
         single_ref[m] = one(facing == step)
     lane = iota((16, ROWS), 1)
-    transfer = ((iota((16, ROWS), 0) - ((lane & 63) >> 2)) & 15) + ((lane >> 6) << 4)
+    transfer = mom_index(iota((16, ROWS), 0)) - mom_index((lane & 63) >> 2)
+    transfer = (transfer & 15) + ((lane >> 6) << 4)
     weights = jnp.zeros((16, ROWS), F32)
     for m in range(4):
         for q in range(16):
@@ -305,6 +320,8 @@
         pltpu.VMEM((2, ORD, ORD), BF16),
         pltpu.VMEM((2, ORD, 2 * ORD), BF16),
         pltpu.VMEM((3, ORD, NX), BF16),
+        pltpu.VMEM((12, 128, 128), BF16),
+        pltpu.VMEM((12, 128, NO), BF16),
         pltpu.SemaphoreType.DMA((6,)),
     ]
     f = call(blocks_kernel, [(ATOMS, 4, 3 * NX)], [HBM, HBM, HBM], scratch, limit=32)
@@ -336,29 +353,31 @@
 def per_device(retarded, injection, neighbours, bond_count, bond_mode, mode_shift, occupation, coupling):
     sent = blocks_of(neighbours, retarded[0, 0], injection[0, 0])
     selectors, weights = prepared(bond_count, bond_mode, mode_shift, occupation, coupling[0])
-    pieces = exchange(sent, "en")
-    spread = exchange(image_of(selectors, pieces), "mom")
-    back = exchange(convolved(weights, spread), "mom")
+    pieces = exchange(sent, ("y_hi", "z", "core"))
+    spread = exchange(image_of(selectors, pieces), ("y_lo", "x"))
+    back = exchange(convolved(weights, spread), ("y_lo", "x"))
     out = call(unpack_kernel, [(ATOMS, 4, NX)], [VMEM], kind=F32)(back)
     return out[None, None]
 
 
 def solution(mesh):
-    en = P("en")
+    axes = ("x", "y_lo", "z", "y_hi", "core")
+    mesh = Mesh(mesh.devices.reshape(8, 2, 8, 4, 2), axes)
+    mom, en = axes[:2], axes[2:]
     in_specs = (
-        P("mom", "en", None, None, None),
-        P("mom", "en", None, None, None),
+        P(mom, en, None, None, None),
+        P(mom, en, None, None, None),
         P(),
-        en,
-        P("en", None),
+        P(en),
+        P(en, None),
         P(),
         P(),
-        P("en", None, None, None),
+        P(en, None, None, None),
     )
     return jax.shard_map(
         per_device,
         mesh=mesh,
         in_specs=in_specs,
-        out_specs=P("mom", "en", None, None, None),
+        out_specs=P(mom, en, None, None, None),
         check_vma=False,
     )

time: 78.6 us -> 77.4 us (0.985); the launches traced: 78.3 us -> 75.8 us
  waiting for transfers between devices: 12.8 us -> 11.1 us
    all_to_all x1, waiting for transfers between devices: 12.8 us -> 11.1 us  [exchange(): return lax.all_to_all(x, axis, split_axis=0, concat_axis=0, tiled=True)]
  transfers between devices with their start and end apart: 1 -> 1, of which waited for: 1 -> 1; matrix products, arithmetic and copies ran while one was open for 0% -> 0% of each run, Pallas kernels for 2% -> 3%
where the time goes in v5:
time: 77.4 us; the launch traced here: 75.8 us
  blocking collectives  28.8 us (37%)
  starting transfers between devices  24.5 us (32%)
  waiting for transfers between devices  11.1 us (14%)
  Pallas kernels  10.7 us (14%)
    all_to_all x2, blocking collectives, exchange(): return lax.all_to_all(x, axis, split_axis=0, concat_axis=0, tiled=True)  28.8 us
    all_to_all x1, starting transfers between devices, exchange(): return lax.all_to_all(x, axis, split_axis=0, concat_axis=0, tiled=True)  24.5 us
    all_to_all x1, waiting for transfers between devices, exchange(): return lax.all_to_all(x, axis, split_axis=0, concat_axis=0, tiled=True)  11.1 us
    pallas_call x1, Pallas kernels, blocks_of(): f(*(pltpu.with_memory_space_constraint(x, pltpu.HBM) for x in operands))  6.14 us
    pallas_call x1, Pallas kernels, prepared(): outs = f(bond_count, bond_mode, mode_shift, occupation.T, coupling)  1.91 us
  transfers between devices with their start and end apart: 1, of which 1 were waited for; matrix products, arithmetic and copies ran while one was open for 0% of the time, Pallas kernels for 3%

profile of v5, /device:TPU:1, one launch (start us, length us, event | category | flops | bytes accessed | tf_op | source)
XLA Modules:
  0.0 75.8 jit_solution(13070677346416766186)
XLA Ops:
  0.0 0.0 copy-start.3
  0.0 0.0 copy-start
  0.0 0.0 copy-start.2
  0.0 0.0 copy-start.1
  0.0 6.1 %shard_map.83 = bf16[64,4,432]{2,1,0:T(4,128)(2,1)} custom-call(s32[4,64]{1,0:T(4,128)} %bitcast.14, bf16[12,2,768]{2,1,0:T(2,128)(2,1)} %bitcast.13, bf16[2,768,768]{2,1,0:T(8,128)(2,1)} %bitcast.12), custom_call_target="tpu_custom_call" | custom-call | tf_op jit(solution)/shard_map/pallas_call | solution.py:329
  6.2 24.5 %all-to-all-start = ((bf16[64,4,432]{2,1,0:T(4,128)(2,1)}), bf16[64,4,432]{2,1,0:T(4,128)(2,1)S(1)}, u32[]{:S(2)}, u32[]{:S(2)}) async-start(bf16[64,4,432]{2,1,0:T(4,128)(2,1)} %shard_map.83), calls=%async_computation | async-start | bytes 524288 | tf_op jit(solution)/shard_map/all_to_all | solution.py:350
  31.3 0.0 copy-done.3
  31.3 0.0 copy-done
  31.3 0.0 copy-done.2
  31.3 0.0 copy-done.1
  31.3 1.9 %shard_map.82 = (bf16[576,256]{1,0:T(8,128)(2,1)S(1)}, bf16[256,256]{1,0:T(8,128)(2,1)S(1)}, bf16[4,256,256]{2,1,0:T(8,128)(2,1)S(1)}, bf16[4,256,256]{2,1,0:T(8...) custom-call(s32[1]{0:T(128)S(6)} %copy.12.count_ref, ...), custom_call_target="tpu_custom_call" | custom-call | tf_op jit(solution)/shard_map/pallas_call | solution.py:337
  33.3 11.1 %all-to-all-done.p_ref = bf16[64,4,432]{2,1,0:T(4,128)(2,1)S(1)} async-done(((bf16[64,4,432]{2,1,0:T(4,128)(2,1)}), bf16[64,4,432]{2,1,0:T(4,128)(2,1)S(1)}, u32[]{:S(2)}, u32[]{:S(2)}) %all-to-all-start) | async-done | bytes 221216 | tf_op jit(solution)/shard_map/all_to_all | solution.py:350
  44.3 1.1 %shard_map.84 = bf16[16,4,2304]{2,1,0:T(4,128)(2,1)S(1)} custom-call(bf16[576,256]{1,0:T(8,128)(2,1)S(1)} %get-tuple-element.16.kron_ref, bf16[256,256]{1,0:T(8,128)(2,1)S(1)} %get-tuple-element.17.turn_ref, bf16[4,256,256]{2,1,0:T(8,128)(2,1)S(1)} %get-tuple-element.18.part_ref, bf16[4,256,256]{2,1,0:T(8,128)(2,1)S(1)} %get-tuple-element.19.pair_ref, ...), custom_call_target="tpu_custom_call" | custom-call | tf_op jit(solution)/shard_map/pallas_call | solution.py:342
  45.5 15.9 %all_to_all.15.v_ref = bf16[16,4,2304]{2,1,0:T(4,128)(2,1)S(1)} all-to-all(bf16[16,4,2304]{2,1,0:T(4,128)(2,1)S(1)} %shard_map.84), channel_id=1, replica_groups=mesh['x'=8,'y_lo'=2,'z'=8,'y_hi'=4,'core'=2] {'y_lo','x'}, dimensions={0} | all-to-all | bytes 589824 | tf_op jit(solution)/shard_map/all_to_all | solution.py:350
  61.4 0.6 shard_map.85
  62.0 12.9 %all_to_all.16.x_ref = bf16[16,4,576]{2,1,0:T(4,128)(2,1)S(1)} all-to-all(bf16[16,4,576]{2,1,0:T(4,128)(2,1)S(1)} %shard_map.85), channel_id=1, replica_groups=mesh['x'=8,'y_lo'=2,'z'=8,'y_hi'=4,'core'=2] {'y_lo','x'}, dimensions={0} | all-to-all | bytes 147456 | tf_op jit(solution)/shard_map/all_to_all | solution.py:350
  74.9 1.0 %shard_map.86 = f32[64,4,144]{2,1,0:T(4,128)} custom-call(bf16[16,4,576]{2,1,0:T(4,128)(2,1)S(1)} %all_to_all.16.x_ref), custom_call_target="tpu_custom_call" | custom-call | tf_op jit(solution)/shard_map/pallas_call | solution.py:359
  (1 shorter events, 0.0 us)
Async XLA Ops:
  0.0 31.3 %copy-start.3 = (f32[1,4,12,12]{3,1,2,0:T(4,128)S(1)}, f32[1,4,12,12]{3,1,2,0:T(4,128)}, u32[]{:S(2)}) copy-start(f32[1,4,12,12]{3,1,2,0:T(4,128)} %param.15) | copy-start | bytes 6916
  0.0 31.3 %copy-start = (f32[16,6]{0,1:T(8,128)S(1)}, f32[16,6]{0,1:T(8,128)}, u32[]{:S(2)}) copy-start(f32[16,6]{0,1:T(8,128)} %param.14) | copy-start | bytes 1156
  0.0 31.3 %copy-start.2 = (s32[6]{0:T(128)S(1)}, s32[6]{0:T(128)}, u32[]{:S(2)}) copy-start(s32[6]{0:T(128)} %shift_ref.1) | copy-start | bytes 76
  0.0 31.3 %copy-start.1 = (s32[1,4]{1,0:T(1,128)S(1)}, s32[1,4]{1,0:T(1,128)}, u32[]{:S(2)}) copy-start(s32[1,4]{1,0:T(1,128)} %mode_ref.1) | copy-start | bytes 52
  6.2 38.2 %all-to-all-start = ((bf16[64,4,432]{2,1,0:T(4,128)(2,1)}), bf16[64,4,432]{2,1,0:T(4,128)(2,1)S(1)}, u32[]{:S(2)}, u32[]{:S(2)}) async-start(bf16[64,4,432]{2,1,0:T(4,128)(2,1)} %shard_map.83), calls=%async_computation | async-start | bytes 524288 | tf_op jit(solution)/shard_map/all_to_all | solution.py:350

commit v6 on v5

--- a/solution.py
+++ b/solution.py
@@ -45,6 +45,10 @@
 
 def mom_index(place):
     return ((place & 7) << 1) + (place >> 3)
+
+
+def energy_of(row):
+    return (mom_index(row >> 2) << 2) + (row & 3)
 
 
 def blocks_kernel(nb_hbm, s_hbm, g_hbm, out_ref, nb_ref, s_ref, g_ref, left_ref, z_ref, mask_ref, pick_ref, sems):
@@ -184,7 +188,7 @@
         factors.append(dot(one(column == source), jnp.concatenate([high, middle, low], axis=0)))
     kron_ref[...] = (factors[0] * factors[1]).astype(BF16)
     row, column = iota((ROWS, ROWS), 0), iota((ROWS, ROWS), 1)
-    turn_ref[...] = one(column == (en_place(row & 63) << 2) + (row >> 6))
+    turn_ref[...] = one(column == (en_place(energy_of(row & 63)) << 2) + (row >> 6))
     x = iota((1, WIN), 1)
     swapped = NO * orbital_of(x) + atom_of(x)
     below = orbital_of(x) < atom_of(x)
@@ -196,7 +200,7 @@
     part_ref[2] = jnp.where(below, kept, jnp.where(x == swapped, 0.0, -turned)).astype(BF16)
     part_ref[3] = jnp.where(below, turned, kept).astype(BF16)
     part = (row >> 6) - (column >> 6)
-    gap = (column & 63) - (row & 63)
+    gap = energy_of(column & 63) - energy_of(row & 63)
     alone = jnp.abs(jnp.where(part == 0, gap, 8 * ROWS))
     facing = jnp.where((row & 128) > 0, -gap, gap)
     facing = jnp.where((part == 0) | (part == 2), facing, 8 * ROWS)
@@ -205,7 +209,7 @@
         pair_ref[m] = one(alone == step)
         single_ref[m] = one(facing == step)
     lane = iota((16, ROWS), 1)
-    transfer = mom_index(iota((16, ROWS), 0)) - mom_index((lane & 63) >> 2)
+    transfer = iota((16, ROWS), 0) - mom_index((lane & 63) >> 2)
     transfer = (transfer & 15) + ((lane >> 6) << 4)
     weights = jnp.zeros((16, ROWS), F32)
     for m in range(4):
@@ -355,7 +359,7 @@
     selectors, weights = prepared(bond_count, bond_mode, mode_shift, occupation, coupling[0])
     pieces = exchange(sent, ("y_hi", "z", "core"))
     spread = exchange(image_of(selectors, pieces), ("y_lo", "x"))
-    back = exchange(convolved(weights, spread), ("y_lo", "x"))
+    back = exchange(convolved(weights, spread), ("x", "y_lo"))
     out = call(unpack_kernel, [(ATOMS, 4, NX)], [VMEM], kind=F32)(back)
     return out[None, None]
 

time: 77.4 us -> 78 us (level)
  the two profiles are of different devices: /device:TPU:1 before, /device:TPU:32 now
where the time goes in v6:
time: 78 us; the launch traced here: 77.8 us
  blocking collectives  31.2 us (40%)
  starting transfers between devices  23.1 us (30%)
  waiting for transfers between devices  11.9 us (15%)
  Pallas kernels  10.7 us (14%)
    all_to_all x2, blocking collectives, exchange(): return lax.all_to_all(x, axis, split_axis=0, concat_axis=0, tiled=True)  31.2 us
    all_to_all x1, starting transfers between devices, exchange(): return lax.all_to_all(x, axis, split_axis=0, concat_axis=0, tiled=True)  23.1 us
    all_to_all x1, waiting for transfers between devices, exchange(): return lax.all_to_all(x, axis, split_axis=0, concat_axis=0, tiled=True)  11.9 us
    pallas_call x1, Pallas kernels, blocks_of(): f(*(pltpu.with_memory_space_constraint(x, pltpu.HBM) for x in operands))  6.14 us
    pallas_call x1, Pallas kernels, prepared(): outs = f(bond_count, bond_mode, mode_shift, occupation.T, coupling)  1.92 us
  transfers between devices with their start and end apart: 1, of which 1 were waited for; matrix products, arithmetic and copies ran while one was open for 0% of the time, Pallas kernels for 2%

profile of v6, /device:TPU:32, one launch (start us, length us, event | category | flops | bytes accessed | tf_op | source)
XLA Modules:
  0.0 77.8 jit_solution(15340331289999213966)
XLA Ops:
  0.0 0.0 copy-start.3
  0.0 0.0 copy-start
  0.0 0.0 copy-start.2
  0.0 0.0 copy-start.1
  0.0 6.1 %shard_map.83 = bf16[64,4,432]{2,1,0:T(4,128)(2,1)} custom-call(s32[4,64]{1,0:T(4,128)} %bitcast.14, bf16[12,2,768]{2,1,0:T(2,128)(2,1)} %bitcast.13, bf16[2,768,768]{2,1,0:T(8,128)(2,1)} %bitcast.12), custom_call_target="tpu_custom_call" | custom-call | tf_op jit(solution)/shard_map/pallas_call | solution.py:333
  6.2 23.1 %all-to-all-start = ((bf16[64,4,432]{2,1,0:T(4,128)(2,1)}), bf16[64,4,432]{2,1,0:T(4,128)(2,1)S(1)}, u32[]{:S(2)}, u32[]{:S(2)}) async-start(bf16[64,4,432]{2,1,0:T(4,128)(2,1)} %shard_map.83), calls=%async_computation | async-start | bytes 524288 | tf_op jit(solution)/shard_map/all_to_all | solution.py:354
  29.9 0.0 copy-done.3
  29.9 0.0 copy-done
  29.9 0.0 copy-done.2
  29.9 0.0 copy-done.1
  30.0 1.9 %shard_map.82 = (bf16[576,256]{1,0:T(8,128)(2,1)S(1)}, bf16[256,256]{1,0:T(8,128)(2,1)S(1)}, bf16[4,256,256]{2,1,0:T(8,128)(2,1)S(1)}, bf16[4,256,256]{2,1,0:T(8...) custom-call(s32[1]{0:T(128)S(6)} %copy.12.count_ref, ...), custom_call_target="tpu_custom_call" | custom-call | tf_op jit(solution)/shard_map/pallas_call | solution.py:341
  31.9 11.9 %all-to-all-done.p_ref = bf16[64,4,432]{2,1,0:T(4,128)(2,1)S(1)} async-done(((bf16[64,4,432]{2,1,0:T(4,128)(2,1)}), bf16[64,4,432]{2,1,0:T(4,128)(2,1)S(1)}, u32[]{:S(2)}, u32[]{:S(2)}) %all-to-all-start) | async-done | bytes 221216 | tf_op jit(solution)/shard_map/all_to_all | solution.py:354
  43.8 1.1 %shard_map.84 = bf16[16,4,2304]{2,1,0:T(4,128)(2,1)S(1)} custom-call(bf16[576,256]{1,0:T(8,128)(2,1)S(1)} %get-tuple-element.16.kron_ref, bf16[256,256]{1,0:T(8,128)(2,1)S(1)} %get-tuple-element.17.turn_ref, bf16[4,256,256]{2,1,0:T(8,128)(2,1)S(1)} %get-tuple-element.18.part_ref, bf16[4,256,256]{2,1,0:T(8,128)(2,1)S(1)} %get-tuple-element.19.pair_ref, ...), custom_call_target="tpu_custom_call" | custom-call | tf_op jit(solution)/shard_map/pallas_call | solution.py:346
  45.0 17.7 %all_to_all.15.v_ref = bf16[16,4,2304]{2,1,0:T(4,128)(2,1)S(1)} all-to-all(bf16[16,4,2304]{2,1,0:T(4,128)(2,1)S(1)} %shard_map.84), channel_id=1, replica_groups=mesh['x'=8,'y_lo'=2,'z'=8,'y_hi'=4,'core'=2] {'y_lo','x'}, dimensions={0} | all-to-all | bytes 589824 | tf_op jit(solution)/shard_map/all_to_all | solution.py:354
  62.7 0.6 shard_map.85
  63.3 13.5 %all_to_all.16.x_ref = bf16[16,4,576]{2,1,0:T(4,128)(2,1)S(1)} all-to-all(bf16[16,4,576]{2,1,0:T(4,128)(2,1)S(1)} %shard_map.85), channel_id=1, replica_groups=mesh['x'=8,'y_lo'=2,'z'=8,'y_hi'=4,'core'=2] {'x','y_lo'}, dimensions={0} | all-to-all | bytes 147456 | tf_op jit(solution)/shard_map/all_to_all | solution.py:354
  76.8 1.0 %shard_map.86 = f32[64,4,144]{2,1,0:T(4,128)} custom-call(bf16[16,4,576]{2,1,0:T(4,128)(2,1)S(1)} %all_to_all.16.x_ref), custom_call_target="tpu_custom_call" | custom-call | tf_op jit(solution)/shard_map/pallas_call | solution.py:363
  (1 shorter events, 0.0 us)
Async XLA Ops:
  0.0 29.9 %copy-start.3 = (f32[1,4,12,12]{3,1,2,0:T(4,128)S(1)}, f32[1,4,12,12]{3,1,2,0:T(4,128)}, u32[]{:S(2)}) copy-start(f32[1,4,12,12]{3,1,2,0:T(4,128)} %param.15) | copy-start | bytes 6916
  0.0 29.9 %copy-start = (f32[16,6]{0,1:T(8,128)S(1)}, f32[16,6]{0,1:T(8,128)}, u32[]{:S(2)}) copy-start(f32[16,6]{0,1:T(8,128)} %param.14) | copy-start | bytes 1156
  0.0 29.9 %copy-start.2 = (s32[6]{0:T(128)S(1)}, s32[6]{0:T(128)}, u32[]{:S(2)}) copy-start(s32[6]{0:T(128)} %shift_ref.1) | copy-start | bytes 76
  0.0 29.9 %copy-start.1 = (s32[1,4]{1,0:T(1,128)S(1)}, s32[1,4]{1,0:T(1,128)}, u32[]{:S(2)}) copy-start(s32[1,4]{1,0:T(1,128)} %mode_ref.1) | copy-start | bytes 52
  6.2 37.7 %all-to-all-start = ((bf16[64,4,432]{2,1,0:T(4,128)(2,1)}), bf16[64,4,432]{2,1,0:T(4,128)(2,1)S(1)}, u32[]{:S(2)}, u32[]{:S(2)}) async-start(bf16[64,4,432]{2,1,0:T(4,128)(2,1)} %shard_map.83), calls=%async_computation | async-start | bytes 524288 | tf_op jit(solution)/shard_map/all_to_all | solution.py:354
